TPU v7x, 32 devices: a whole 2x2x4 slice. The times are simulated.
32 devices in a mesh: ctx: 8 (over z, x), ch: 4 (over y, core).
Axes of the slice: x: 2, y: 2, z: 4, core: 2. Of those that a mesh axis runs over, the one named last changes fastest.
Arguments:
- query_input: bfloat16 [4096, 4096], P('ch', 'ctx'), may hold values from -6 to 6
- key_input: bfloat16 [4096, 4096], P('ch', 'ctx'), may hold values from -6 to 6
- value_input: bfloat16 [4096, 4096], P('ch', 'ctx'), may hold values from -6 to 6
- decay_rate: float32 [8, 16], P('ch'), may hold values from 0 to 1, as said below
- residue: float32 [8, 16], P('ch'), may hold values from -1 to 1
- doc_ends: int32 [4], replicated, may hold values from 1 to 4096, as said below
- out_weight: bfloat16 [4096, 4096], P(None, 'ch'), may hold values from -0.09375 to 0.09375
- out_cotangent: bfloat16 [4096, 4096], P('ctx', 'ch'), may hold values from -6 to 6
Outputs:
- query_grad: bfloat16 [4096, 4096], P('ch', 'ctx')
- key_grad: bfloat16 [4096, 4096], P('ch', 'ctx')
- value_grad: bfloat16 [4096, 4096], P('ch', 'ctx')
- weight_grad: float32 [4096, 4096], P('ctx', 'ch')
Inputs may be any that keep to these rules, and one draw needn't show every extreme that they name: `doc_ends`: strictly increasing; the last entry equals 4096. `decay_rate`: positive.
All inputs are finite; a program needn't handle non-finite values.
Results may differ from a plain program's by a relative error of at most 0.0029.
Values may be sent and summed in bfloat16 or wider, within the bound.
A program may use at most 128 MiB of HBM per device.

v0:
```python
import math

import jax
import jax.numpy as jnp
from jax import lax
from jax.sharding import PartitionSpec as P


def passed_along(block, axis, distance):
    devices = range(lax.axis_size(axis))
    route = [(i - distance, i) for i in devices if i - distance in devices]
    return lax.ppermute(block, axis, route)


def local(
    query_input, key_input, value_input, decay_rate, residue, doc_ends, out_weight, out_cotangent
):
    rows_here, length = query_input.shape
    groups = decay_rate.shape[0]
    group_rows = rows_here // groups
    shard_index = lax.axis_index("ctx")
    anchor = shard_index * length
    offsets = jnp.arange(length, dtype=jnp.int32)
    positions = anchor + offsets
    doc_ids = jnp.sum((doc_ends[None, :] <= positions[:, None]).astype(jnp.int32), axis=1)
    previous = jnp.where(shard_index > 0, jnp.sum((doc_ends <= anchor - 1).astype(jnp.int32)), -1)
    row_block = out_weight
    output_grad = lax.psum_scatter(
        lax.dot_general(
            row_block, out_cotangent, (((1,), (1,)), ((), ())), preferred_element_type=jnp.float32
        ),
        "ch",
        scatter_dimension=0,
        tiled=True,
    )
    highest = lax.Precision.HIGHEST
    place = offsets.astype(jnp.float32)
    centre = place - 0.5 * length
    rising = jnp.exp(-centre[None, :, None] * decay_rate[:, None, :]) * residue[:, None, :]
    falling = jnp.exp(centre[None, :, None] * decay_rate[:, None, :])
    kernel = jnp.einsum("gtn,gsn->gts", rising, falling, precision=highest)
    causal = (offsets[:, None] >= offsets[None, :]) & (doc_ids[:, None] == doc_ids[None, :])
    kernel = jnp.where(causal[None, :, :], kernel, 0.0)
    alive_mask = (doc_ids == previous).astype(jnp.float32)
    tail_mask = (doc_ids == doc_ids[-1]).astype(jnp.float32)
    carry_in_map = (
        residue[:, :, None]
        * jnp.exp(-decay_rate[:, :, None] * (place + 1.0)[None, None, :])
        * alive_mask[None, None, :]
    )
    carry_out_map = (
        jnp.exp(-decay_rate[:, :, None] * (length - 1.0 - place)[None, None, :])
        * tail_mask[None, None, :]
    )
    back_out_map = (
        jnp.exp(-decay_rate[:, :, None] * place[None, None, :]) * alive_mask[None, None, :]
    )
    back_in_map = (
        residue[:, :, None]
        * jnp.exp(-decay_rate[:, :, None] * (length - place)[None, None, :])
        * tail_mask[None, None, :]
    )
    transit = jnp.exp(-decay_rate * length) * (doc_ids[-1] == previous).astype(jnp.float32)
    query_f = query_input.astype(jnp.float32)
    key_f = key_input.astype(jnp.float32)
    value_f = value_input.astype(jnp.float32)
    mixed = (key_f * value_f).reshape(groups, group_rows, length)
    signal = (output_grad * query_f).reshape(groups, group_rows, length)
    forward_part = jnp.einsum("gnl,gcl->gnc", carry_out_map, mixed, precision=highest)
    backward_part = jnp.einsum("gnl,gcl->gnc", back_out_map, signal, precision=highest)

    def chain_turn(turn_index, carried):
        ahead, behind = carried
        ahead = passed_along(transit[:, :, None] * ahead + forward_part, "ctx", 1)
        behind = passed_along(transit[:, :, None] * behind + backward_part, "ctx", -1)
        return (ahead, behind)

    start_pair = (jnp.zeros_like(forward_part), jnp.zeros_like(backward_part))
    entering, returning = lax.fori_loop(0, lax.axis_size("ctx") - 1, chain_turn, start_pair)
    filtered = jnp.einsum("gcs,gts->gct", mixed, kernel, precision=highest)
    filtered = filtered + jnp.einsum("gnc,gnt->gct", entering, carry_in_map, precision=highest)
    spread = jnp.einsum("gct,gts->gcs", signal, kernel, precision=highest)
    spread = spread + jnp.einsum("gnc,gns->gcs", returning, back_in_map, precision=highest)
    filtered = filtered.reshape(rows_here, length)
    spread = spread.reshape(rows_here, length)
    gated = (query_f * filtered).astype(jnp.bfloat16)
    query_grad = (output_grad * filtered).astype(jnp.bfloat16)
    key_grad = (spread * value_f).astype(jnp.bfloat16)
    value_grad = (spread * key_f).astype(jnp.bfloat16)
    gathered = lax.all_gather(gated, "ch", axis=0, tiled=True)
    norm_factor = 1.0 / math.sqrt(length * lax.axis_size("ctx"))
    row_block = gathered
    weight_grad = lax.psum_scatter(
        jnp.dot(row_block, out_cotangent, preferred_element_type=jnp.float32) * norm_factor,
        "ctx",
        scatter_dimension=0,
        tiled=True,
    )
    return (query_grad, key_grad, value_grad, weight_grad)


def solution(mesh):
    return jax.shard_map(
        local,
        mesh=mesh,
        in_specs=(
            P("ch", "ctx"),
            P("ch", "ctx"),
            P("ch", "ctx"),
            P("ch", None),
            P("ch", None),
            P(),
            P(None, "ch"),
            P("ctx", "ch"),
        ),
        out_specs=(P("ch", "ctx"), P("ch", "ctx"), P("ch", "ctx"), P("ctx", "ch")),
        check_vma=False,
    )
```

profile of v0, /device:TPU:24, one launch (start us, length us, event | category | flops | bytes accessed | tf_op | source)
XLA Modules:
  0.0 518.1 jit_solution(614125705850805751)
XLA Ops:
  8.4 10.2 %fusion.70 = f32[4096,512]{1,0:T(8,128)} fusion(bf16[4096,1024]{1,0:T(8,128)(2,1)} %param.16, bf16[512,1024]{1,0:T(8,128)(2,1)S(1)} %copy-done), kind=kOutput, calls=%fused_computation.83 | convolution fusion | flops 4294967296 | bytes 17825792 | tf_op jit(solution)/shard_map/dot_general | solution.py:29
  23.4 3.3 fusion.37
  28.3 2.5 fusion.33
  30.8 60.7 %reduce-scatter.3.cloned.1.call-done = f32[1024,512]{1,0:T(8,128)} async-done(((f32[4096,512]{1,0:T(8,128)}), f32[1024,512]{1,0:T(8,128)}) %reduce-scatter.3.cloned.1.call-update) | async-done | bytes 2097168 | tf_op jit(solution)/shard_map/reduce_scatter | solution.py:28
  91.5 2.2 convert_multiply_fusion.1
  93.7 2.5 fusion.29
  96.2 75.8 %while.12 = (s32[]{:T(128)}, f32[2,16,512]{2,1,0:T(8,128)S(1)}, f32[2,16,512]{2,1,0:T(8,128)S(1)}, f32[2,16]{1,0:T(2,128)S(1)}, f32[2,16,512]{2,1,0:T(8,128)}, /*index=5*/f32[2,16,512]{2,1,0:T(8,128)}, s32[]{:T(128)}) while((s32[]{:T(128)}, f32[2,16,512]{2,1,0:T(8,128)S(1)}, f32[2,16,512]{2,1,0:T(8,128)S(1)}, f32[2,16]{1,0:T(2,128)S(1)}, ...), condition=%wide.region_4.5_spmd, body=%wide.region_3.4_spmd.sunk | while | flops 65538 | bytes 917789 | solution.py:79
  97.8 3.4 collective-permute-start
  101.2 3.4 collective-permute-start.1
  105.1 2.5 collective-permute-done.1
  109.1 1.9 collective-permute-start
  111.0 4.8 collective-permute-start.1
  121.6 5.1 collective-permute-start.1
  132.3 5.1 collective-permute-start.1
  143.1 5.1 collective-permute-start.1
  153.9 5.1 collective-permute-start.1
  164.7 5.2 collective-permute-start.1
  172.0 2.7 fusion.24
  174.8 5.4 %fusion.8 = f32[2,512,512]{2,1,0:T(8,128)S(1)} fusion(f32[2,512,512]{2,1,0:T(8,128)S(1)} %fusion.24, f32[2,512,512]{2,1,0:T(8,128)S(1)} %bitcast.24, f32[2,512,512]{2,1,0:T(8,128)} %fusion.37, pred[512,512]{1,0:T(8,128)(4,1)S(1)} %fusion.16), kind=kOutput, calls=%fused_computation.17 | convolution fusion | flops 3222274048 | bytes 8650752 | tf_op jit(solution)/shard_map/gcs,gts->gct/dot_general | solution.py:80
  180.2 2.0 fusion.2
  182.5 37.5 %all-gather.2.cloned.1.call-done = bf16[4096,512]{1,0:T(8,128)(2,1)} async-done(((bf16[1024,512]{1,0:T(8,128)(2,1)}), bf16[4096,512]{1,0:T(8,128)(2,1)}) %all-gather.2.cloned.1.call-update) | async-done | bytes 4194320 | tf_op jit(solution)/shard_map/all_gather | solution.py:90
  219.9 10.3 %broadcast_multiply_fusion = f32[4096,1024]{1,0:T(8,128)} fusion(bf16[4096,512]{1,0:T(8,128)(2,1)} %all-gather.2.cloned.1.call-done, bf16[512,1024]{1,0:T(8,128)(2,1)S(1)} %copy-done), kind=kOutput, calls=%fused_computation.2 | convolution fusion | flops 4299161600 | bytes 22020096 | tf_op jit(solution)/shard_map/dot_general | solution.py:94
  232.8 3.7 fusion.11
  238.4 273.1 %reduce-scatter.5.cloned.1.call-done = f32[512,1024]{1,0:T(8,128)} async-done(((f32[4096,1024]{1,0:T(8,128)}), f32[512,1024]{1,0:T(8,128)}) %reduce-scatter.5.cloned.1.call-update) | async-done | bytes 2097168 | tf_op jit(solution)/shard_map/reduce_scatter | solution.py:93
  (76 shorter events, 45.2 us)
Async XLA Ops:
  7.2 84.3 %reduce-scatter.3.cloned.1.call-start = ((), (), s32[]{:S(2)}) async-start(), calls=%async_computation.2 | async-start | bytes 10485760 | tf_op jit(solution)/shard_map/reduce_scatter | solution.py:28
  18.6 3.8 copy-start.12
  18.6 4.7 copy-start.10
  18.7 8.0 %copy-start.6 = (bf16[1024,512]{1,0:T(8,128)(2,1)S(1)}, bf16[1024,512]{1,0:T(8,128)(2,1)}, u32[]{:S(2)}) copy-start(bf16[1024,512]{1,0:T(8,128)(2,1)} %param.12) | copy-start | bytes 3145732
  18.7 8.0 %copy-start.8 = (bf16[1024,512]{1,0:T(8,128)(2,1)S(1)}, bf16[1024,512]{1,0:T(8,128)(2,1)}, u32[]{:S(2)}) copy-start(bf16[1024,512]{1,0:T(8,128)(2,1)} %param.11) | copy-start | bytes 3145732
  18.7 201.3 %all-gather.2.cloned.1.call-start = ((), (), s32[]{:S(2)}) async-start(), calls=%async_computation.3 | async-start | bytes 5242880 | tf_op jit(solution)/shard_map/all_gather | solution.py:90
  97.8 7.3 %collective-permute-start = (f32[2,16,512]{2,1,0:T(8,128)}, f32[2,16,512]{2,1,0:T(8,128)S(1)}, u32[]{:S(2)}, u32[]{:S(2)}) collective-permute-start(f32[2,16,512]{2,1,0:T(8,128)} %get-tuple-element.102), channel_id=1, source_target_pairs={{0,4},{4,8},{8,12},{12,16},{16,20},{20,24},{24,28},{1,5},{5,9},{9,... | collective-permute-start | bytes 196616 | tf_op jit(solution)/shard_map/while/body/eval_jaxpr/ppermute | solution.py:12
  101.2 6.4 %collective-permute-start.1 = (f32[2,16,512]{2,1,0:T(8,128)}, f32[2,16,512]{2,1,0:T(8,128)S(1)}, u32[]{:S(2)}, u32[]{:S(2)}) collective-permute-start(f32[2,16,512]{2,1,0:T(8,128)} %get-tuple-element.103), channel_id=1, source_target_pairs={{4,0},{8,4},{12,8},{16,12},{20,16},{24,20},{28,24},{5,1},{9,5},{13... | collective-permute-start | bytes 196616 | tf_op jit(solution)/shard_map/while/body/eval_jaxpr/ppermute | solution.py:12
  109.1 7.3 %collective-permute-start = (f32[2,16,512]{2,1,0:T(8,128)}, f32[2,16,512]{2,1,0:T(8,128)S(1)}, u32[]{:S(2)}, u32[]{:S(2)}) collective-permute-start(f32[2,16,512]{2,1,0:T(8,128)} %get-tuple-element.102), channel_id=1, source_target_pairs={{0,4},{4,8},{8,12},{12,16},{16,20},{20,24},{24,28},{1,5},{5,9},{9,... | collective-permute-start | bytes 196616 | tf_op jit(solution)/shard_map/while/body/eval_jaxpr/ppermute | solution.py:12
  111.0 7.0 %collective-permute-start.1 = (f32[2,16,512]{2,1,0:T(8,128)}, f32[2,16,512]{2,1,0:T(8,128)S(1)}, u32[]{:S(2)}, u32[]{:S(2)}) collective-permute-start(f32[2,16,512]{2,1,0:T(8,128)} %get-tuple-element.103), channel_id=1, source_target_pairs={{4,0},{8,4},{12,8},{16,12},{20,16},{24,20},{28,24},{5,1},{9,5},{13... | collective-permute-start | bytes 196616 | tf_op jit(solution)/shard_map/while/body/eval_jaxpr/ppermute | solution.py:12
  119.7 7.5 %collective-permute-start = (f32[2,16,512]{2,1,0:T(8,128)}, f32[2,16,512]{2,1,0:T(8,128)S(1)}, u32[]{:S(2)}, u32[]{:S(2)}) collective-permute-start(f32[2,16,512]{2,1,0:T(8,128)} %get-tuple-element.102), channel_id=1, source_target_pairs={{0,4},{4,8},{8,12},{12,16},{16,20},{20,24},{24,28},{1,5},{5,9},{9,... | collective-permute-start | bytes 196616 | tf_op jit(solution)/shard_map/while/body/eval_jaxpr/ppermute | solution.py:12
  121.6 7.3 %collective-permute-start.1 = (f32[2,16,512]{2,1,0:T(8,128)}, f32[2,16,512]{2,1,0:T(8,128)S(1)}, u32[]{:S(2)}, u32[]{:S(2)}) collective-permute-start(f32[2,16,512]{2,1,0:T(8,128)} %get-tuple-element.103), channel_id=1, source_target_pairs={{4,0},{8,4},{12,8},{16,12},{20,16},{24,20},{28,24},{5,1},{9,5},{13... | collective-permute-start | bytes 196616 | tf_op jit(solution)/shard_map/while/body/eval_jaxpr/ppermute | solution.py:12
  130.4 7.5 %collective-permute-start = (f32[2,16,512]{2,1,0:T(8,128)}, f32[2,16,512]{2,1,0:T(8,128)S(1)}, u32[]{:S(2)}, u32[]{:S(2)}) collective-permute-start(f32[2,16,512]{2,1,0:T(8,128)} %get-tuple-element.102), channel_id=1, source_target_pairs={{0,4},{4,8},{8,12},{12,16},{16,20},{20,24},{24,28},{1,5},{5,9},{9,... | collective-permute-start | bytes 196616 | tf_op jit(solution)/shard_map/while/body/eval_jaxpr/ppermute | solution.py:12
  132.3 7.3 %collective-permute-start.1 = (f32[2,16,512]{2,1,0:T(8,128)}, f32[2,16,512]{2,1,0:T(8,128)S(1)}, u32[]{:S(2)}, u32[]{:S(2)}) collective-permute-start(f32[2,16,512]{2,1,0:T(8,128)} %get-tuple-element.103), channel_id=1, source_target_pairs={{4,0},{8,4},{12,8},{16,12},{20,16},{24,20},{28,24},{5,1},{9,5},{13... | collective-permute-start | bytes 196616 | tf_op jit(solution)/shard_map/while/body/eval_jaxpr/ppermute | solution.py:12
  141.2 7.5 %collective-permute-start = (f32[2,16,512]{2,1,0:T(8,128)}, f32[2,16,512]{2,1,0:T(8,128)S(1)}, u32[]{:S(2)}, u32[]{:S(2)}) collective-permute-start(f32[2,16,512]{2,1,0:T(8,128)} %get-tuple-element.102), channel_id=1, source_target_pairs={{0,4},{4,8},{8,12},{12,16},{16,20},{20,24},{24,28},{1,5},{5,9},{9,... | collective-permute-start | bytes 196616 | tf_op jit(solution)/shard_map/while/body/eval_jaxpr/ppermute | solution.py:12
  143.1 7.3 %collective-permute-start.1 = (f32[2,16,512]{2,1,0:T(8,128)}, f32[2,16,512]{2,1,0:T(8,128)S(1)}, u32[]{:S(2)}, u32[]{:S(2)}) collective-permute-start(f32[2,16,512]{2,1,0:T(8,128)} %get-tuple-element.103), channel_id=1, source_target_pairs={{4,0},{8,4},{12,8},{16,12},{20,16},{24,20},{28,24},{5,1},{9,5},{13... | collective-permute-start | bytes 196616 | tf_op jit(solution)/shard_map/while/body/eval_jaxpr/ppermute | solution.py:12
  152.0 7.5 %collective-permute-start = (f32[2,16,512]{2,1,0:T(8,128)}, f32[2,16,512]{2,1,0:T(8,128)S(1)}, u32[]{:S(2)}, u32[]{:S(2)}) collective-permute-start(f32[2,16,512]{2,1,0:T(8,128)} %get-tuple-element.102), channel_id=1, source_target_pairs={{0,4},{4,8},{8,12},{12,16},{16,20},{20,24},{24,28},{1,5},{5,9},{9,... | collective-permute-start | bytes 196616 | tf_op jit(solution)/shard_map/while/body/eval_jaxpr/ppermute | solution.py:12
  153.9 7.3 %collective-permute-start.1 = (f32[2,16,512]{2,1,0:T(8,128)}, f32[2,16,512]{2,1,0:T(8,128)S(1)}, u32[]{:S(2)}, u32[]{:S(2)}) collective-permute-start(f32[2,16,512]{2,1,0:T(8,128)} %get-tuple-element.103), channel_id=1, source_target_pairs={{4,0},{8,4},{12,8},{16,12},{20,16},{24,20},{28,24},{5,1},{9,5},{13... | collective-permute-start | bytes 196616 | tf_op jit(solution)/shard_map/while/body/eval_jaxpr/ppermute | solution.py:12
  162.7 7.6 %collective-permute-start = (f32[2,16,512]{2,1,0:T(8,128)}, f32[2,16,512]{2,1,0:T(8,128)S(1)}, u32[]{:S(2)}, u32[]{:S(2)}) collective-permute-start(f32[2,16,512]{2,1,0:T(8,128)} %get-tuple-element.102), channel_id=1, source_target_pairs={{0,4},{4,8},{8,12},{12,16},{16,20},{20,24},{24,28},{1,5},{5,9},{9,... | collective-permute-start | bytes 196616 | tf_op jit(solution)/shard_map/while/body/eval_jaxpr/ppermute | solution.py:12
  164.7 7.4 %collective-permute-start.1 = (f32[2,16,512]{2,1,0:T(8,128)}, f32[2,16,512]{2,1,0:T(8,128)S(1)}, u32[]{:S(2)}, u32[]{:S(2)}) collective-permute-start(f32[2,16,512]{2,1,0:T(8,128)} %get-tuple-element.103), channel_id=1, source_target_pairs={{4,0},{8,4},{12,8},{16,12},{20,16},{24,20},{28,24},{5,1},{9,5},{13... | collective-permute-start | bytes 196616 | tf_op jit(solution)/shard_map/while/body/eval_jaxpr/ppermute | solution.py:12
  174.7 5.4 %copy-start.4 = (f32[1024,512]{1,0:T(8,128)S(1)}, f32[1024,512]{1,0:T(8,128)}, u32[]{:S(2)}) copy-start(f32[1024,512]{1,0:T(8,128)} %reduce-scatter.3.cloned.1.call-done) | copy-start | bytes 6291460
  174.8 5.4 %copy-start.5 = (bf16[1024,512]{1,0:T(8,128)(2,1)S(1)}, bf16[1024,512]{1,0:T(8,128)(2,1)}, u32[]{:S(2)}) copy-start(bf16[1024,512]{1,0:T(8,128)(2,1)} %param.10) | copy-start | bytes 3145732
  182.2 329.4 %reduce-scatter.5.cloned.1.call-start = ((), (), s32[]{:S(2)}) async-start(), calls=%async_computation.4 | async-start | bytes 18874368 | tf_op jit(solution)/shard_map/reduce_scatter | solution.py:93
  232.8 3.7 copy-start.7
  (7 other events, 12.8 us)
Sparse Core Ops, SparseCore 0:
  18.8 72.6 reduce-scatter.2
  182.3 37.5 all-gather.1
  230.4 281.1 reduce-scatter.4
where the time goes:
time: 522 us; the launch traced here: 518 us
  waiting for transfers between devices  388 us (74%)
  starting transfers between devices  48.9 us (9%)
  matrix products  42.5 us (8%)
  other arithmetic  19.5 us (4%)
  between operations  15.3 us (3%)
    reduce_scatter x1, waiting for transfers between devices, local(): lax.psum_scatter(jnp.dot(row_block, out_cotangent, preferred_element_type...  273 us
    reduce_scatter x1, waiting for transfers between devices, local(): lax.psum_scatter(lax.dot_general(row_block, out_cotangent, (((1,), (1,)),...  60.7 us
    ppermute x14, starting transfers between devices, passed_along(): return lax.ppermute(block, axis, route)  48.4 us
    all_gather x1, waiting for transfers between devices, local(): gathered = lax.all_gather(gated, 'ch', axis=0, tiled=True)  37.5 us
    ppermute x14, waiting for transfers between devices, passed_along(): return lax.ppermute(block, axis, route)  16.2 us
    add x7, other arithmetic, chain_turn(): transit[:, :, None] * behind + backward_part  11.1 us
  transfers between devices with their start and end apart: 17, of which 17 were waited for; matrix products, arithmetic and copies ran while one was open for 3% of the time, Pallas kernels for 0%

commit v1 on v0

v1 whole, which is shorter than its diff:
```python
import math

import jax
import jax.numpy as jnp
from jax import lax
from jax.sharding import PartitionSpec as P

HIGH = lax.Precision.HIGH
TILE = 128


def doc_of(doc_ends, positions):
    return jnp.sum((doc_ends[None, :] <= positions[:, None]).astype(jnp.int32), axis=1)


def local_kernel(decay_rate, residue, doc_ids, length):
    groups = decay_rate.shape[0]
    place = jnp.arange(length, dtype=jnp.float32)
    narrow = jnp.arange(TILE, dtype=jnp.float32)
    half = 0.5 * TILE
    rising = jnp.exp(-decay_rate[:, None, :] * (place - half)[None, :, None]) * residue[:, None, :]
    falling = jnp.exp(decay_rate[:, None, :] * (narrow - half)[None, :, None])
    strip = jnp.einsum("gtn,gsn->gts", rising, falling, precision=lax.Precision.HIGHEST)
    columns = []
    for start in range(0, length, TILE):
        top = jnp.zeros((groups, start, TILE), jnp.float32)
        columns.append(jnp.concatenate([top, strip[:, : length - start]], axis=1))
    kernel = jnp.concatenate(columns, axis=2)
    offsets = jnp.arange(length, dtype=jnp.int32)
    causal = (offsets[:, None] >= offsets[None, :]) & (doc_ids[:, None] == doc_ids[None, :])
    return jnp.where(causal[None], kernel, 0.0)


def exchange_rows(gated, n_ctx, n_ch):
    rows, length = gated.shape
    mine = rows * n_ch // n_ctx
    pieces = gated.reshape(n_ctx // n_ch, n_ch, mine // n_ch, length)
    pieces = lax.all_to_all(pieces, "ch", split_axis=1, concat_axis=0, tiled=True)
    pieces = pieces.reshape(n_ctx, mine // n_ch, length)
    pieces = lax.all_to_all(pieces, "ctx", split_axis=0, concat_axis=0, tiled=True)
    pieces = pieces.transpose(1, 0, 2).reshape(mine // n_ch, n_ctx * length)
    return lax.all_gather(pieces, "ch", axis=0, tiled=True)


def local(
    query_input, key_input, value_input, decay_rate, residue, doc_ends, out_weight, out_cotangent
):
    rows_here, length = query_input.shape
    n_ctx, n_ch = lax.axis_size("ctx"), lax.axis_size("ch")
    groups = decay_rate.shape[0]
    group_rows = rows_here // groups
    me = lax.axis_index("ctx")
    offsets = jnp.arange(length, dtype=jnp.int32)
    place = offsets.astype(jnp.float32)
    doc_ids = doc_of(doc_ends, me * length + offsets)
    blocks = jnp.arange(n_ctx, dtype=jnp.int32)
    last_ids = doc_of(doc_ends, (blocks + 1) * length - 1)
    previous = jnp.where(me > 0, jnp.sum((doc_ends <= me * length - 1).astype(jnp.int32)), -1)
    last = doc_ids[-1]

    cotangent_all = lax.all_gather(out_cotangent, "ctx", axis=0, tiled=True)

    alive_mask = (doc_ids == previous).astype(jnp.float32)
    tail_mask = (doc_ids == last).astype(jnp.float32)
    rate = decay_rate[:, :, None]
    carry_in_map = residue[:, :, None] * jnp.exp(-rate * (place + 1.0)) * alive_mask
    carry_out_map = jnp.exp(-rate * (length - 1.0 - place)) * tail_mask
    back_out_map = jnp.exp(-rate * place) * alive_mask
    back_in_map = residue[:, :, None] * jnp.exp(-rate * (length - place)) * tail_mask
    steps_ahead = me - 1 - blocks
    joined_ahead = (steps_ahead >= 0) & (last_ids == previous)
    ahead_weight = jnp.where(
        joined_ahead[:, None, None],
        jnp.exp(-decay_rate[None] * (length * jnp.maximum(steps_ahead, 0)).astype(jnp.float32)[:, None, None]),
        0.0,
    )
    steps_back = blocks - 1 - me
    before_ids = jnp.concatenate([jnp.full((1,), -1, jnp.int32), last_ids[:-1]])
    joined_back = (steps_back >= 0) & (before_ids == last)
    back_weight = jnp.where(
        joined_back[:, None, None],
        jnp.exp(-decay_rate[None] * (length * jnp.maximum(steps_back, 0)).astype(jnp.float32)[:, None, None]),
        0.0,
    )

    key_f = key_input.astype(jnp.float32)
    value_f = value_input.astype(jnp.float32)
    query_f = query_input.astype(jnp.float32)
    mixed = (key_f * value_f).reshape(groups, group_rows, length)
    forward_part = jnp.einsum("gnl,gcl->gnc", carry_out_map, mixed, precision=HIGH)
    forward_all = lax.all_gather(forward_part, "ctx", axis=0)
    entering = jnp.sum(ahead_weight[..., None] * forward_all, axis=0)

    partial_grad = lax.dot_general(
        out_weight, out_cotangent, (((1,), (1,)), ((), ())), preferred_element_type=jnp.float32
    )
    output_grad = lax.psum_scatter(partial_grad, "ch", scatter_dimension=0, tiled=True)

    kernel = local_kernel(decay_rate, residue, doc_ids, length)
    filtered = jnp.einsum("gcs,gts->gct", mixed, kernel, precision=HIGH)
    filtered = filtered + jnp.einsum("gnc,gnt->gct", entering, carry_in_map, precision=HIGH)
    filtered = filtered.reshape(rows_here, length)
    gated = (query_f * filtered).astype(jnp.bfloat16)
    gated_rows = exchange_rows(gated, n_ctx, n_ch)

    signal = (output_grad * query_f).reshape(groups, group_rows, length)
    backward_part = jnp.einsum("gnl,gcl->gnc", back_out_map, signal, precision=HIGH)
    backward_all = lax.all_gather(backward_part, "ctx", axis=0)
    query_grad = (output_grad * filtered).astype(jnp.bfloat16)
    spread = jnp.einsum("gct,gts->gcs", signal, kernel, precision=HIGH)
    returning = jnp.sum(back_weight[..., None] * backward_all, axis=0)
    spread = spread + jnp.einsum("gnc,gns->gcs", returning, back_in_map, precision=HIGH)
    spread = spread.reshape(rows_here, length)
    key_grad = (spread * value_f).astype(jnp.bfloat16)
    value_grad = (spread * key_f).astype(jnp.bfloat16)

    norm_factor = 1.0 / math.sqrt(length * n_ctx)
    weight_grad = jnp.dot(gated_rows, cotangent_all, preferred_element_type=jnp.float32) * norm_factor
    return (query_grad, key_grad, value_grad, weight_grad)


def solution(mesh):
    return jax.shard_map(
        local,
        mesh=mesh,
        in_specs=(
            P("ch", "ctx"),
            P("ch", "ctx"),
            P("ch", "ctx"),
            P("ch", None),
            P("ch", None),
            P(),
            P(None, "ch"),
            P("ctx", "ch"),
        ),
        out_specs=(P("ch", "ctx"), P("ch", "ctx"), P("ch", "ctx"), P("ctx", "ch")),
        check_vma=False,
    )
```

time: 522 us -> 228 us (0.44)
  waiting for transfers between devices: 388 us -> 34.7 us
  blocking collectives: 0 us -> 131 us
  starting transfers between devices: 48.9 us -> 0.12 us
  other arithmetic: 19.5 us -> 8.84 us
  matrix products: 42.5 us -> 32.4 us
    reduce_scatter x2 -> x1, waiting for transfers between devices: 334 us -> 31.4 us  [local(): lax.psum_scatter(partial_grad, 'ch', scatter_dimension=0, tiled=True)]
    all_to_all x0 -> x2, blocking collectives: none -> 70.2 us  [the longest x1 53.3 us: exchange_rows(): lax.all_to_all(pieces, 'ctx', split_axis=0, concat_axis=0, tiled=True)]
    all_gather x0 -> x2, blocking collectives: none -> 60.4 us  [the longest x1 30.3 us: local(): forward_all = lax.all_gather(forward_part, 'ctx', axis=0)]
    ppermute x14 -> x0, starting transfers between devices: 48.4 us -> none  [passed_along(): return lax.ppermute(block, axis, route)]
    all_gather x1 -> x2, waiting for transfers between devices: 37.5 us -> 2.74 us  [the longest x1 2.74 us: exchange_rows(): return lax.all_gather(pieces, 'ch', axis=0, tiled=True)]
    ppermute x14 -> x0, waiting for transfers between devices: 16.2 us -> none  [passed_along(): return lax.ppermute(block, axis, route)]
    add x8 -> x1, other arithmetic: 11.1 us -> 0.01 us  [local(): doc_ids = doc_of(doc_ends, me * length + offsets)]
    dot_general x9, matrix products: 42.5 us -> 32.4 us  [the longest x1 11.4 us: local(): lax.dot_general(out_weight, out_cotangent, (((1,), (1,)), ((), ())), pref...]
  transfers between devices with their start and end apart: 17 -> 3, of which waited for: 17 -> 2; matrix products, arithmetic and copies ran while one was open for 3% -> 9% of each run, Pallas kernels for 0% -> 0%
where the time goes in v1:
time: 228 us; the launch traced here: 226 us
  blocking collectives  131 us (57%)
  waiting for transfers between devices  34.7 us (15%)
  matrix products  32.4 us (14%)
  between operations  16.6 us (7%)
  other arithmetic  8.84 us (4%)
  local copies, waits for them, and re-layouts  2.62 us (1%)
    all_to_all x1, blocking collectives, exchange_rows(): lax.all_to_all(pieces, 'ctx', split_axis=0, concat_axis=0, tiled=True)  53.3 us
    reduce_scatter x1, waiting for transfers between devices, local(): lax.psum_scatter(partial_grad, 'ch', scatter_dimension=0, tiled=True)  31.4 us
    all_gather x1, blocking collectives, local(): forward_all = lax.all_gather(forward_part, 'ctx', axis=0)  30.3 us
    all_gather x1, blocking collectives, local(): backward_all = lax.all_gather(backward_part, 'ctx', axis=0)  30 us
    all_to_all x1, blocking collectives, exchange_rows(): lax.all_to_all(pieces, 'ch', split_axis=1, concat_axis=0, tiled=True)  16.9 us
    dot_general x1, matrix products, local(): lax.dot_general(out_weight, out_cotangent, (((1,), (1,)), ((), ())), pref...  11.4 us
    dot_general x1, matrix products, local(): jnp.dot(gated_rows, cotangent_all, preferred_element_type=jnp.float32)  10.5 us
  transfers between devices with their start and end apart: 3, of which 2 were waited for; matrix products, arithmetic and copies ran while one was open for 9% of the time, Pallas kernels for 0%

profile of v1, /device:TPU:24, one launch (start us, length us, event | category | flops | bytes accessed | tf_op | source)
XLA Modules:
  0.0 225.8 jit_solution(17652264326971221755)
XLA Ops:
  8.0 11.4 %fusion.67 = f32[4096,512]{1,0:T(8,128)} fusion(bf16[4096,1024]{1,0:T(8,128)(2,1)} %param.14, bf16[512,1024]{1,0:T(8,128)(2,1)} %param.15), kind=kOutput, calls=%fused_computation.103 | convolution fusion | flops 4294967296 | bytes 17825792 | tf_op jit(solution)/shard_map/dot_general | solution.py:94
  19.6 0.5 all-gather.7.cloned.1.call-update
  20.2 0.7 fusion.28
  21.2 0.6 slice.18
  21.7 0.6 fusion.56
  23.2 0.7 compare_and_fusion
  23.9 0.6 compare_convert_fusion
  25.0 0.9 fusion.24
  25.9 30.3 %all-gather = f32[16,16,512]{2,1,0:T(8,128)S(1)} all-gather(f32[2,16,512]{2,1,0:T(8,128)S(1)} %fusion.24), channel_id=2, replica_groups=mesh['ctx'=8,'ch'=4] {'ctx'}, dimensions={0}, use_global_device_ids=true | all-gather | bytes 589824 | tf_op jit(solution)/shard_map/all_gather | solution.py:91
  56.7 1.9 fusion.10
  58.6 2.4 %convolution_add_fusion.1 = f32[2,512,512]{2,1,0:T(8,128)} fusion(f32[2,512,512]{2,1,0:T(8,128)S(1)} %fusion.10, f32[2,16,512]{2,1,0:T(8,128)S(1)} %multiply_reduce_fusion.1, f32[512]{0:T(512)S(1)} %get-tuple-element.9, f32[512]{0:T(512)S(1)} %fusion.54, f32[2,16]{1,0:T(2,128)S(1)} %copy-done.15, f32[2,16]{1,0:T(2,128)S(1)} %neg.5), kind=kOutput, calls=%fused_computation.22 | convolution fusion | flops 50905088 | bytes 4264192 | tf_op jit(solution)/shard_map/gnc,gnt->gct/dot_general | solution.py:101
  61.0 31.4 %reduce-scatter.2.cloned.1.call-done = f32[1024,512]{1,0:T(8,128)} async-done(((f32[4096,512]{1,0:T(8,128)}), f32[1024,512]{1,0:T(8,128)}) %reduce-scatter.2.cloned.1.call-update) | async-done | bytes 2097168 | tf_op jit(solution)/shard_map/reduce_scatter | solution.py:97
  92.4 3.9 %fusion.2 = (bf16[1024,512]{1,0:T(8,128)(2,1)S(1)}, bf16[1024,512]{1,0:T(8,128)(2,1)}, f32[1024,512]{1,0:T(8,128)S(1)}) fusion(bf16[1024,512]{1,0:T(8,128)(2,1)S(1)} %copy-done.6, f32[2,512,512]{2,1,0:T(8,128)} %convolution_add_fusion.1, f32[1024,512]{1,0:T(8,128)} %reduce-scatter.2.cloned.1.call-done), kind=kLoop, calls=%fused_computation.11 | loop fusion | flops 3145728 | bytes 9437184 | tf_op jit(solution)/shard_map/convert_element_type | solution.py:103
  96.4 16.9 %all_to_all.20 = bf16[2,4,128,512]{3,2,0,1:T(8,128)(2,1)S(1)} all-to-all(bf16[2,4,128,512]{3,2,0,1:T(8,128)(2,1)S(1)} %copy.24), channel_id=1, replica_groups=mesh['ctx'=8,'ch'=4] {'ch'}, dimensions={1} | all-to-all | bytes 2097152 | tf_op jit(solution)/shard_map/all_to_all | solution.py:38
  113.3 53.3 %all_to_all.21 = bf16[8,128,512]{2,1,0:T(8,128)(2,1)S(1)} all-to-all(bf16[8,128,512]{2,1,0:T(8,128)(2,1)S(1)} %bitcast.38), channel_id=1, replica_groups=mesh['ctx'=8,'ch'=4] {'ctx'}, dimensions={0} | all-to-all | bytes 2097152 | tf_op jit(solution)/shard_map/all_to_all | solution.py:40
  166.6 1.3 copy.25
  167.9 1.7 fusion.16
  169.7 30.0 %all-gather.1 = f32[16,16,512]{2,1,0:T(8,128)S(1)} all-gather(f32[2,16,512]{2,1,0:T(8,128)S(1)} %fusion.16), channel_id=3, replica_groups=mesh['ctx'=8,'ch'=4] {'ctx'}, dimensions={0}, use_global_device_ids=true | all-gather | bytes 589824 | tf_op jit(solution)/shard_map/all_gather | solution.py:108
  199.9 1.9 fusion.8
  201.8 1.0 convolution_add_fusion
  203.0 0.3 copy-done.3
  203.3 1.9 fusion
  205.2 2.7 %all-gather.5.cloned.1.call-done = bf16[512,4096]{0,1:T(8,128)(2,1)} async-done(((bf16[128,4096]{0,1:T(8,128)(2,1)}), bf16[512,4096]{0,1:T(8,128)(2,1)}) %all-gather.5.cloned.1.call-update) | async-done | bytes 4194320 | tf_op jit(solution)/shard_map/all_gather | solution.py:42
  207.9 10.5 %convolution_multiply_fusion = f32[512,1024]{1,0:T(8,128)} fusion(bf16[512,4096]{0,1:T(8,128)(2,1)} %all-gather.5.cloned.1.call-done, bf16[4096,1024]{1,0:T(8,128)(2,1)} %all-gather.7.cloned.1.call-done), kind=kOutput, calls=%fused_computation.23 | convolution fusion | flops 4295491584 | bytes 14680064 | tf_op jit(solution)/shard_map/dot_general | solution.py:118
  (64 shorter events, 1.6 us)
Async XLA Ops:
  8.0 84.4 %reduce-scatter.2.cloned.1.call-start = ((), (), s32[]{:S(2)}) async-start(), calls=%async_computation.3 | async-start | bytes 10485760 | tf_op jit(solution)/shard_map/reduce_scatter | solution.py:97
  19.5 0.7 copy-start.17
  19.5 0.7 copy-start.14
  19.5 1.6 copy-start.18
  19.5 5.2 %copy-start = (bf16[1024,512]{1,0:T(8,128)(2,1)S(1)}, bf16[1024,512]{1,0:T(8,128)(2,1)}, u32[]{:S(2)}) copy-start(bf16[1024,512]{1,0:T(8,128)(2,1)} %param.10) | copy-start | bytes 3145732
  19.5 5.2 %copy-start.2 = (bf16[1024,512]{1,0:T(8,128)(2,1)S(1)}, bf16[1024,512]{1,0:T(8,128)(2,1)}, u32[]{:S(2)}) copy-start(bf16[1024,512]{1,0:T(8,128)(2,1)} %param.9) | copy-start | bytes 3145732
  19.5 185.7 %all-gather.7.cloned.1.call-start = ((), (), s32[]{:S(2)}) async-start(), calls=%async_computation.5 | async-start | bytes 9437184 | tf_op jit(solution)/shard_map/all_gather | solution.py:61
  20.1 187.8 %all-gather.5.cloned.1.call-start = ((), (), s32[]{:S(2)}) async-start(), calls=%async_computation.4 | async-start | bytes 5242880 | tf_op jit(solution)/shard_map/all_gather | solution.py:42
  20.9 35.7 %copy-start.4 = (f32[2,512,128]{1,2,0:T(8,128)}, f32[2,512,128]{1,2,0:T(8,128)S(1)}, u32[]{:S(2)}) copy-start(f32[2,512,128]{1,2,0:T(8,128)S(1)} %fusion.28) | copy-start | bytes 1572868
  21.0 35.7 %copy-start.11 = (f32[2,128,128]{1,2,0:T(8,128)}, f32[2,128,128]{1,2,0:T(8,128)S(1)}, u32[]{:S(2)}) copy-start(f32[2,128,128]{1,2,0:T(8,128)S(1)} %slice.22) | copy-start | bytes 393220
  21.0 35.6 %copy-start.7 = (f32[2,256,128]{1,2,0:T(8,128)}, f32[2,256,128]{1,2,0:T(8,128)S(1)}, u32[]{:S(2)}) copy-start(f32[2,256,128]{1,2,0:T(8,128)S(1)} %slice.21) | copy-start | bytes 786436
  24.5 34.0 %copy-start.13 = (f32[512]{0:T(512)}, f32[512]{0:T(512)S(1)}, u32[]{:S(2)}) copy-start(f32[512]{0:T(512)S(1)} %get-tuple-element.9) | copy-start | bytes 6148
  56.6 1.9 copy-start.9
  56.6 1.9 copy-start.15
  58.6 33.8 %copy-start.6 = (bf16[1024,512]{1,0:T(8,128)(2,1)S(1)}, bf16[1024,512]{1,0:T(8,128)(2,1)}, u32[]{:S(2)}) copy-start(bf16[1024,512]{1,0:T(8,128)(2,1)} %param.8) | copy-start | bytes 3145732
  167.9 32.0 %copy-start.5 = (f32[2,512,128]{1,2,0:T(8,128)S(1)}, f32[2,512,128]{1,2,0:T(8,128)}, u32[]{:S(2)}) copy-start(f32[2,512,128]{1,2,0:T(8,128)} %copy-done.4) | copy-start | bytes 1572868
  167.9 32.0 %copy-start.8 = (f32[2,256,128]{1,2,0:T(8,128)S(1)}, f32[2,256,128]{1,2,0:T(8,128)}, u32[]{:S(2)}) copy-start(f32[2,256,128]{1,2,0:T(8,128)} %copy-done.7) | copy-start | bytes 786436
  167.9 32.0 %copy-start.12 = (f32[2,128,128]{1,2,0:T(8,128)S(1)}, f32[2,128,128]{1,2,0:T(8,128)}, u32[]{:S(2)}) copy-start(f32[2,128,128]{1,2,0:T(8,128)} %copy-done.11) | copy-start | bytes 393220
  167.9 32.0 %copy-start.10 = (pred[512,512]{0,1:T(8,128)(4,1)S(1)}, pred[512,512]{0,1:T(8,128)(4,1)}, u32[]{:S(2)}) copy-start(pred[512,512]{0,1:T(8,128)(4,1)} %copy-done.9) | copy-start | bytes 786436
  199.9 1.9 copy-start.16
  201.8 1.2 copy-start.1
  201.8 1.5 copy-start.3
Sparse Core Ops, SparseCore 0:
  19.6 72.6 reduce-scatter.1
Sparse Core Ops, SparseCore 1:
  22.4 147.4 all-gather.6
  171.8 36.0 all-gather.4

commit v2 on v1

--- a/solution.py
+++ b/solution.py
@@ -1,12 +1,17 @@
+import functools
 import math
 
 import jax
 import jax.numpy as jnp
 from jax import lax
+from jax.experimental import pallas as pl
+from jax.experimental.pallas import tpu as pltpu
 from jax.sharding import PartitionSpec as P
 
+MESH = pl.DeviceIdType.MESH
 HIGH = lax.Precision.HIGH
 TILE = 128
+CUT = 96
 
 
 def doc_of(doc_ends, positions):
@@ -42,6 +47,274 @@
     return lax.all_gather(pieces, "ch", axis=0, tiled=True)
 
 
+def ctx_id(index):
+    return (index, lax.axis_index("ch"))
+
+
+def ch_id(index):
+    return (lax.axis_index("ctx"), index)
+
+
+def remote(src, dst, send, recv, device):
+    return pltpu.make_async_remote_copy(
+        src_ref=src, dst_ref=dst, send_sem=send, recv_sem=recv, device_id=device, device_id_type=MESH
+    )
+
+
+def greet(devices):
+    barrier = pltpu.get_barrier_semaphore()
+    for device in devices:
+        pl.semaphore_signal(barrier, inc=1, device_id=device, device_id_type=MESH)
+    pl.semaphore_wait(barrier, len(devices))
+
+
+def state_kernel(n_ctx, sign, part_ref, all_ref, send, recv):
+    me = lax.axis_index("ctx")
+    greet([ctx_id(lax.rem(me + d, n_ctx)) for d in range(1, n_ctx)])
+
+    def inside(index):
+        return (index >= 0) & (index < n_ctx)
+
+    for d in range(1, n_ctx):
+        to = me + sign * d
+
+        @pl.when(inside(to))
+        def _():
+            remote(part_ref, all_ref.at[me], send.at[d], recv.at[d], ctx_id(to)).start()
+
+    for d in range(1, n_ctx):
+        to, came = me + sign * d, me - sign * d
+
+        @pl.when(inside(came))
+        def _():
+            remote(part_ref, all_ref.at[came], send.at[d], recv.at[d], ctx_id(came)).wait_recv()
+
+        @pl.when(inside(to))
+        def _():
+            remote(part_ref, all_ref.at[me], send.at[d], recv.at[d], ctx_id(to)).wait_send()
+
+
+def spread_states(part, sign, number):
+    n_ctx = lax.axis_size("ctx")
+    if n_ctx != 8:
+        return lax.all_gather(part, "ctx", axis=0)
+    any_space = pl.BlockSpec(memory_space=pl.ANY)
+    return pl.pallas_call(
+        functools.partial(state_kernel, n_ctx, sign),
+        out_shape=jax.ShapeDtypeStruct((n_ctx,) + part.shape, part.dtype),
+        in_specs=[any_space],
+        out_specs=any_space,
+        scratch_shapes=[pltpu.SemaphoreType.DMA((n_ctx,)), pltpu.SemaphoreType.DMA((n_ctx,))],
+        compiler_params=pltpu.CompilerParams(collective_id=number, has_side_effects=True),
+        name="states_ahead" if sign > 0 else "states_back",
+    )(part)
+
+
+def move_kernel(
+    cut, cot_ref, gated_ref, cots_ref, rows_ref, turned_ref, joined_ref,
+    own_sem, f_recv, g_recv, q_recv, f_send, g_send, p_send, q_send,
+    turn_send, turn_recv, join_send, join_recv, wide_send, wide_recv,
+):
+    me, ch = lax.axis_index("ctx"), lax.axis_index("ch")
+    z, x = me // 2, me % 2
+    twin = me + 1 - 2 * x
+    y, core = ch // 2, ch % 2
+    across = (1 - y) * 2 + core
+    mate = y * 2 + 1 - core
+    length = cot_ref.shape[0]
+    piece = turned_ref.shape[1]
+    greet(
+        [ctx_id(lax.rem(me + d, 8)) for d in range(1, 8)]
+        + [ch_id(lax.rem(ch + d, 4)) for d in range(1, 4)]
+    )
+    first, rest = pl.ds(0, cut), pl.ds(cut, length - cut)
+
+    turns = []
+    for d in range(1, 4):
+        to = lax.rem(ch + d, 4)
+        came = lax.rem(ch + 4 - d, 4)
+        for h in range(2):
+            slot = 2 * d + h
+            out = remote(
+                gated_ref.at[h, to], turned_ref.at[2 * ch + h], turn_send.at[slot], turn_recv.at[slot], ch_id(to)
+            )
+            out.start()
+            back = remote(
+                gated_ref.at[h, to], turned_ref.at[2 * came + h], turn_send.at[slot], turn_recv.at[slot], ch_id(to)
+            )
+            turns.append((out, back))
+    locals_ = [pltpu.make_async_copy(gated_ref.at[h, ch], turned_ref.at[2 * ch + h], own_sem.at[h]) for h in range(2)]
+    locals_.append(pltpu.make_async_copy(cot_ref, cots_ref.at[me], own_sem.at[2]))
+
+    def to_twin_first():
+        return remote(cot_ref.at[first], cots_ref.at[me, first], p_send.at[0], g_recv.at[z], ctx_id(twin))
+
+    def to_twin_rest(origin, src):
+        slot = 2 * origin + x
+        return remote(src, cots_ref.at[slot, rest], q_send.at[origin], q_recv.at[origin], ctx_id(twin))
+
+    def along(origin, side, src):
+        slot = 2 * origin + x
+        to = me + 2 * side
+        return remote(src, cots_ref.at[slot], f_send.at[(side + 1) // 2, origin], f_recv.at[origin], ctx_id(to))
+
+    def along_first(origin, side):
+        slot = 2 * origin + 1 - x
+        to = me + 2 * side
+        part = cots_ref.at[slot, first]
+        return remote(part, part, g_send.at[(side + 1) // 2, origin], g_recv.at[origin], ctx_id(to))
+
+    def goes(side):
+        return z < 3 if side > 0 else z > 0
+
+    to_twin_first().start()
+    for side in (1, -1):
+
+        @pl.when(goes(side))
+        def _():
+            along(z, side, cot_ref).start()
+
+    to_twin_rest(z, cot_ref.at[rest]).start()
+    for copy in locals_:
+        copy.start()
+
+    for copy in locals_[:2]:
+        copy.wait()
+    for out, back in turns:
+        back.wait_recv()
+
+    columns = pl.ds(pl.multiple_of(me * length, 128), length)
+    mine = pl.ds(pl.multiple_of(ch * piece, piece), piece)
+    joins = []
+    for d in range(1, 8):
+        to = lax.rem(me + d, 8)
+        came = lax.rem(me + 8 - d, 8)
+        from_columns = pl.ds(pl.multiple_of(came * length, 128), length)
+        out = remote(turned_ref.at[to], joined_ref.at[:, columns], join_send.at[d], join_recv.at[d], ctx_id(to))
+        out.start()
+        back = remote(
+            turned_ref.at[to], joined_ref.at[:, from_columns], join_send.at[d], join_recv.at[d], ctx_id(to)
+        )
+        joins.append((out, back))
+    own_join = pltpu.make_async_copy(turned_ref.at[me], joined_ref.at[:, columns], own_sem.at[3])
+    own_join.start()
+
+    remote(
+        cot_ref.at[first], cots_ref.at[twin, first], p_send.at[0], g_recv.at[z], ctx_id(twin)
+    ).wait_recv()
+    for side in (1, -1):
+
+        @pl.when(goes(side))
+        def _():
+            along_first(z, side).start()
+
+    def step(s):
+        for side in (1, -1):
+            origin = z - side * s
+
+            @pl.when((origin >= 0) & (origin <= 3))
+            def _():
+                slot = 2 * origin + x
+                arrived = cots_ref.at[slot]
+                along(origin, side, arrived).wait_recv()
+
+                @pl.when(goes(side))
+                def _():
+                    along(origin, side, arrived).start()
+
+                to_twin_rest(origin, cots_ref.at[slot, rest]).start()
+
+        for side in (1, -1):
+            origin = z - side * s
+
+            @pl.when((origin >= 0) & (origin <= 3))
+            def _():
+                along_first(origin, side).wait_recv()
+
+                @pl.when(goes(side))
+                def _():
+                    along_first(origin, side).start()
+
+    step(1)
+    own_join.wait()
+    for out, back in joins:
+        back.wait_recv()
+
+    def rows_of(index):
+        return rows_ref.at[pl.ds(pl.multiple_of(index * piece, piece), piece)]
+
+    wide_across = remote(joined_ref, rows_of(ch), wide_send.at[0], wide_recv.at[0], ch_id(across))
+    wide_mate = remote(joined_ref, rows_of(ch), wide_send.at[1], wide_recv.at[1], ch_id(mate))
+    wide_own = pltpu.make_async_copy(joined_ref, rows_of(ch), own_sem.at[4])
+    wide_across.start()
+    wide_mate.start()
+    wide_own.start()
+    step(2)
+    remote(joined_ref, rows_of(across), wide_send.at[0], wide_recv.at[0], ch_id(across)).wait_recv()
+    wide_on = remote(rows_of(across), rows_of(across), wide_send.at[2], wide_recv.at[2], ch_id(mate))
+    wide_on.start()
+    step(3)
+
+    remote(joined_ref, rows_of(mate), wide_send.at[1], wide_recv.at[1], ch_id(mate)).wait_recv()
+    far = (1 - y) * 2 + 1 - core
+    remote(rows_of(across), rows_of(far), wide_send.at[2], wide_recv.at[2], ch_id(mate)).wait_recv()
+    for origin in range(4):
+        slot = 2 * origin + 1 - x
+        part = cots_ref.at[slot, rest]
+        remote(part, part, q_send.at[origin], q_recv.at[origin], ctx_id(twin)).wait_recv()
+    to_twin_first().wait_send()
+    for origin in range(4):
+        to_twin_rest(origin, cot_ref.at[rest]).wait_send()
+        for side in (1, -1):
+
+            @pl.when(goes(side) & (origin <= z if side > 0 else origin >= z))
+            def _():
+                along(origin, side, cot_ref).wait_send()
+                along_first(origin, side).wait_send()
+
+    for out, back in turns + joins:
+        out.wait_send()
+    wide_across.wait_send()
+    wide_mate.wait_send()
+    wide_on.wait_send()
+    wide_own.wait()
+    locals_[2].wait()
+
+
+def move_all(gated, cotangent):
+    n_ctx, n_ch = lax.axis_size("ctx"), lax.axis_size("ch")
+    rows, length = gated.shape
+    if (n_ctx, n_ch) != (8, 4) or rows % (2 * n_ch * 16) or length % 128:
+        return (
+            exchange_rows(gated, n_ctx, n_ch),
+            lax.all_gather(cotangent, "ctx", axis=0, tiled=True),
+        )
+    piece = rows // 2 // n_ch
+    width = cotangent.shape[1]
+    any_space = pl.BlockSpec(memory_space=pl.ANY)
+    bf16 = jnp.bfloat16
+    dma = pltpu.SemaphoreType.DMA
+    cots, gathered, _, _ = pl.pallas_call(
+        functools.partial(move_kernel, CUT),
+        out_shape=(
+            jax.ShapeDtypeStruct((n_ctx, length, width), bf16),
+            jax.ShapeDtypeStruct((rows // 2, n_ctx * length), bf16),
+            jax.ShapeDtypeStruct((n_ctx, piece, length), bf16),
+            jax.ShapeDtypeStruct((piece, n_ctx * length), bf16),
+        ),
+        in_specs=[any_space] * 2,
+        out_specs=[any_space] * 4,
+        scratch_shapes=[
+            dma((5,)), dma((4,)), dma((4,)), dma((4,)), dma((2, 4)), dma((2, 4)), dma((1,)), dma((4,)),
+            dma((8,)), dma((8,)), dma((8,)), dma((8,)), dma((3,)), dma((3,)),
+        ],
+        compiler_params=pltpu.CompilerParams(collective_id=2, has_side_effects=True),
+        cost_estimate=pl.CostEstimate(flops=0, bytes_accessed=300_000_000, transcendentals=0),
+        name="move_all",
+    )(cotangent, gated.reshape(2, n_ch, piece, length))
+    return gathered, cots.reshape(n_ctx * length, width)
+
+
 def local(
     query_input, key_input, value_input, decay_rate, residue, doc_ends, out_weight, out_cotangent
 ):
@@ -58,8 +331,6 @@
     previous = jnp.where(me > 0, jnp.sum((doc_ends <= me * length - 1).astype(jnp.int32)), -1)
     last = doc_ids[-1]
 
-    cotangent_all = lax.all_gather(out_cotangent, "ctx", axis=0, tiled=True)
-
     alive_mask = (doc_ids == previous).astype(jnp.float32)
     tail_mask = (doc_ids == last).astype(jnp.float32)
     rate = decay_rate[:, :, None]
@@ -88,8 +359,10 @@
     query_f = query_input.astype(jnp.float32)
     mixed = (key_f * value_f).reshape(groups, group_rows, length)
     forward_part = jnp.einsum("gnl,gcl->gnc", carry_out_map, mixed, precision=HIGH)
-    forward_all = lax.all_gather(forward_part, "ctx", axis=0)
-    entering = jnp.sum(ahead_weight[..., None] * forward_all, axis=0)
+    forward_all = spread_states(forward_part, 1, 0)
+    entering = jnp.sum(
+        jnp.where(joined_ahead[:, None, None, None], ahead_weight[..., None] * forward_all, 0.0), axis=0
+    )
 
     partial_grad = lax.dot_general(
         out_weight, out_cotangent, (((1,), (1,)), ((), ())), preferred_element_type=jnp.float32
@@ -101,14 +374,17 @@
     filtered = filtered + jnp.einsum("gnc,gnt->gct", entering, carry_in_map, precision=HIGH)
     filtered = filtered.reshape(rows_here, length)
     gated = (query_f * filtered).astype(jnp.bfloat16)
-    gated_rows = exchange_rows(gated, n_ctx, n_ch)
+    gated_rows, cotangent_all = move_all(gated, out_cotangent)
+    output_grad, gated_rows, cotangent_all = lax.optimization_barrier((output_grad, gated_rows, cotangent_all))
 
     signal = (output_grad * query_f).reshape(groups, group_rows, length)
     backward_part = jnp.einsum("gnl,gcl->gnc", back_out_map, signal, precision=HIGH)
-    backward_all = lax.all_gather(backward_part, "ctx", axis=0)
+    backward_all = spread_states(backward_part, -1, 1)
     query_grad = (output_grad * filtered).astype(jnp.bfloat16)
     spread = jnp.einsum("gct,gts->gcs", signal, kernel, precision=HIGH)
-    returning = jnp.sum(back_weight[..., None] * backward_all, axis=0)
+    returning = jnp.sum(
+        jnp.where(joined_back[:, None, None, None], back_weight[..., None] * backward_all, 0.0), axis=0
+    )
     spread = spread + jnp.einsum("gnc,gns->gcs", returning, back_in_map, precision=HIGH)
     spread = spread.reshape(rows_here, length)
     key_grad = (spread * value_f).astype(jnp.bfloat16)

time: 228 us -> 220 us (0.965)
  the two profiles are of different devices: /device:TPU:24 before, /device:TPU:4 now
where the time goes in v2:
time: 220 us; the launch traced here: 219 us
  Pallas kernels  153 us (70%)
  matrix products  30.6 us (14%)
  other arithmetic  15.3 us (7%)
  between operations  15.1 us (7%)
  local copies, waits for them, and re-layouts  4.85 us (2%)
    pallas_call x1, Pallas kernels, move_all(): pl.pallas_call(functools.partial(move_kernel, CUT), out_shape=(jax.ShapeD...  123 us
    pallas_call x2, Pallas kernels, spread_states(): pl.pallas_call(functools.partial(state_kernel, n_ctx, sign), out_shape=ja...  30.1 us
    dot_general x1, matrix products, local(): lax.dot_general(out_weight, out_cotangent, (((1,), (1,)), ((), ())), pref...  11.4 us
    dot_general x1, matrix products, local(): jnp.dot(gated_rows, cotangent_all, preferred_element_type=jnp.float32)  7.99 us
  transfers between devices with their start and end apart: 1, of which 0 were waited for; matrix products, arithmetic and copies ran while one was open for 8% of the time, Pallas kernels for 62%

profile of v2, /device:TPU:4, one launch (start us, length us, event | category | flops | bytes accessed | tf_op | source)
XLA Modules:
  0.0 219.2 jit_solution(2376463857233828241)
XLA Ops:
  7.2 11.4 %fusion.67 = f32[4096,512]{1,0:T(8,128)} fusion(bf16[4096,1024]{1,0:T(8,128)(2,1)} %param.14, bf16[512,1024]{1,0:T(8,128)(2,1)} %cot_ref.1), kind=kOutput, calls=%fused_computation.103 | convolution fusion | flops 4294967296 | bytes 17825792 | tf_op jit(solution)/shard_map/dot_general | solution.py:367
  18.6 0.7 copy-done.20
  19.3 0.7 fusion.28
  20.0 0.8 slice.22
  20.8 0.7 slice.21
  23.6 1.2 compare_convert_fusion
  24.8 1.8 convert_multiply_fusion.1
  26.6 1.6 fusion.24.part_ref
  28.2 13.4 %states_ahead.1 = f32[8,2,16,512]{3,2,1,0:T(8,128)} custom-call(f32[2,16,512]{2,1,0:T(8,128)} %fusion.24.part_ref), custom_call_target="tpu_custom_call" | custom-call | tf_op jit(solution)/shard_map/states_ahead/pallas_call | solution.py:102
  41.7 0.7 compare_and_fusion
  43.0 1.3 select_reduce_fusion.1
  44.6 3.2 %fusion.10 = f32[2,512,512]{2,1,0:T(8,128)S(1)} fusion(f32[2,512,512]{2,1,0:T(8,128)S(1)} %bitcast.25, f32[2,128,128]{1,2,0:T(8,128)} %slice.22, f32[2,256,128]{1,2,0:T(8,128)} %slice.21, f32[2,384,128]{1,2,0:T(8,128)S(1)} %slice.20, f32[2,512,128]{1,2,0:T(8,128)} %copy-done.3, pred[512,512]{0,1:T(8,128)(4,1)S(1)} %fusion.7), kind=kOutput, calls=%fused_computation.29 | convolution fusion | flops 1617952768 | bytes 5767168 | tf_op jit(solution)/shard_map/gcs,gts->gct/dot_general | solution.py:373
  47.8 1.1 convolution_add_fusion.1
  49.0 1.3 fusion
  50.4 123.2 %move_all.1 = (bf16[8,512,1024]{2,1,0:T(8,128)(2,1)}, bf16[512,4096]{1,0:T(8,128)(2,1)}, bf16[8,128,512]{2,1,0:T(8,128)(2,1)}, bf16[128,4096]{1,0:T(8,128)(2,1)}) custom-call(bf16[512,1024]{1,0:T(8,128)(2,1)} %cot_ref.1, bf16[2,4,128,512]{3,2,1,0:T(8,128)(2,1)} %bitcast.28), custom_call_target="tpu_custom_call" | custom-call | bytes 300000000 | tf_op jit(solution)/shard_map/move_all/pallas_call | solution.py:297
  174.7 3.5 %convert_multiply_fusion.3 = (f32[1024,512]{1,0:T(8,128)S(1)}, bf16[1024,512]{1,0:T(8,128)(2,1)}) fusion(f32[1024,512]{1,0:T(8,128)} %reduce-scatter.2.cloned.1.call-done, bf16[1024,512]{1,0:T(8,128)(2,1)} %param.8, f32[2,512,512]{2,1,0:T(8,128)S(1)} %convolution_add_fusion.1), kind=kLoop, calls=%fused_computation.7 | loop fusion | flops 2097152 | bytes 8388608 | tf_op jit(solution)/shard_map/mul | solution.py:380
  178.3 2.0 fusion.8
  180.4 1.6 fusion.16.part_ref
  181.9 16.8 %states_back.1 = f32[8,2,16,512]{3,2,1,0:T(8,128)} custom-call(f32[2,16,512]{2,1,0:T(8,128)} %fusion.16.part_ref), custom_call_target="tpu_custom_call" | custom-call | tf_op jit(solution)/shard_map/states_back/pallas_call | solution.py:102
  198.7 1.2 select_reduce_fusion
  199.9 1.1 convolution_add_fusion
  201.1 1.9 fusion.1
  203.1 1.3 copy-done.22
  204.4 8.0 %convolution_multiply_fusion = f32[512,1024]{1,0:T(8,128)} fusion(bf16[512,4096]{1,0:T(8,128)(2,1)} %get-tuple-element.12, bf16[4096,1024]{1,0:T(8,128)(2,1)S(1)} %bitcast.30), kind=kOutput, calls=%fused_computation.23 | convolution fusion | flops 4295491584 | bytes 14680064 | tf_op jit(solution)/shard_map/dot_general | solution.py:394
  (64 shorter events, 3.8 us)
Async XLA Ops:
  7.2 167.6 %reduce-scatter.2.cloned.1.call-start = ((), (), s32[]{:S(2)}) async-start(), calls=%async_computation.1 | async-start | bytes 10485760 | tf_op jit(solution)/shard_map/reduce_scatter | solution.py:370
  18.6 0.7 copy-start.20
  18.6 0.7 copy-start.13
  19.3 2.3 %copy-start.21 = (s32[4]{0:T(128)S(1)}, s32[4]{0:T(128)}, u32[]{:S(2)}) copy-start(s32[4]{0:T(128)} %param.13) | copy-start | bytes 52
  19.3 5.5 %copy-start = (bf16[1024,512]{1,0:T(8,128)(2,1)S(1)}, bf16[1024,512]{1,0:T(8,128)(2,1)}, u32[]{:S(2)}) copy-start(bf16[1024,512]{1,0:T(8,128)(2,1)} %param.10) | copy-start | bytes 3145732
  20.0 1.5 copy-start.3
  24.8 1.8 copy-start.9
  42.5 0.6 copy-start.18
  44.6 3.2 %copy-start.6 = (pred[512,512]{0,1:T(8,128)(4,1)}, pred[512,512]{0,1:T(8,128)(4,1)S(1)}, u32[]{:S(2)}) copy-start(pred[512,512]{0,1:T(8,128)(4,1)S(1)} %fusion.7) | copy-start | bytes 786436
  44.6 3.2 %copy-start.11 = (f32[512]{0:T(512)S(1)}, f32[512]{0:T(512)}, u32[]{:S(2)}) copy-start(f32[512]{0:T(512)} %get-tuple-element.18) | copy-start | bytes 6148
  44.6 3.2 %copy-start.14 = (f32[2,16]{1,0:T(2,128)S(1)}, f32[2,16]{1,0:T(2,128)}, u32[]{:S(2)}) copy-start(f32[2,16]{1,0:T(2,128)} %param.12) | copy-start | bytes 388
  47.8 1.2 copy-start.2
  174.7 3.5 %copy-start.4 = (f32[2,512,128]{1,2,0:T(8,128)S(1)}, f32[2,512,128]{1,2,0:T(8,128)}, u32[]{:S(2)}) copy-start(f32[2,512,128]{1,2,0:T(8,128)} %copy-done.3) | copy-start | bytes 1572868
  174.7 3.5 %copy-start.5 = (f32[2,256,128]{1,2,0:T(8,128)S(1)}, f32[2,256,128]{1,2,0:T(8,128)}, u32[]{:S(2)}) copy-start(f32[2,256,128]{1,2,0:T(8,128)} %slice.21) | copy-start | bytes 786436
  174.7 3.5 %copy-start.7 = (pred[512,512]{0,1:T(8,128)(4,1)S(1)}, pred[512,512]{0,1:T(8,128)(4,1)}, u32[]{:S(2)}) copy-start(pred[512,512]{0,1:T(8,128)(4,1)} %copy-done.6) | copy-start | bytes 786436
  174.7 3.5 %copy-start.8 = (f32[2,128,128]{1,2,0:T(8,128)S(1)}, f32[2,128,128]{1,2,0:T(8,128)}, u32[]{:S(2)}) copy-start(f32[2,128,128]{1,2,0:T(8,128)} %slice.22) | copy-start | bytes 393220
  178.2 2.0 copy-start.12
  178.3 2.0 copy-start.17
  180.3 18.4 %copy-start.19 = (pred[8]{0:T(512)(128)(4,1)S(1)}, pred[8]{0:T(512)(128)(4,1)}, u32[]{:S(2)}) copy-start(pred[8]{0:T(512)(128)(4,1)} %copy-done.18) | copy-start | bytes 28
  180.3 19.6 %copy-start.10 = (f32[512]{0:T(512)S(1)}, f32[512]{0:T(512)}, u32[]{:S(2)}) copy-start(f32[512]{0:T(512)} %copy-done.9) | copy-start | bytes 6148
  180.3 19.6 %copy-start.15 = (f32[2,16]{1,0:T(2,128)S(1)}, f32[2,16]{1,0:T(2,128)}, u32[]{:S(2)}) copy-start(f32[2,16]{1,0:T(2,128)} %param.12) | copy-start | bytes 388
  180.3 19.6 %copy-start.16 = (f32[512]{0:T(512)S(1)}, f32[512]{0:T(512)}, u32[]{:S(2)}) copy-start(f32[512]{0:T(512)} %fusion.53) | copy-start | bytes 6148
  199.9 1.2 copy-start.1
  199.9 4.5 %copy-start.22 = (bf16[8,512,1024]{2,1,0:T(8,128)(2,1)S(1)}, bf16[8,512,1024]{2,1,0:T(8,128)(2,1)}, u32[]{:S(2)}) copy-start(bf16[8,512,1024]{2,1,0:T(8,128)(2,1)} %get-tuple-element.10) | copy-start | bytes 25165828
Sparse Core Ops, SparseCore 0:
  18.8 82.9 reduce-scatter.1

commit v3 on v2

--- a/solution.py
+++ b/solution.py
@@ -68,50 +68,53 @@
     pl.semaphore_wait(barrier, len(devices))
 
 
-def state_kernel(n_ctx, sign, part_ref, all_ref, send, recv):
+def inside(index):
+    return (index >= 0) & (index < 8)
+
+
+def state_copies(part, slots, send, recv, sign):
     me = lax.axis_index("ctx")
-    greet([ctx_id(lax.rem(me + d, n_ctx)) for d in range(1, n_ctx)])
-
-    def inside(index):
-        return (index >= 0) & (index < n_ctx)
-
-    for d in range(1, n_ctx):
+    for d in range(1, 8):
         to = me + sign * d
 
         @pl.when(inside(to))
         def _():
-            remote(part_ref, all_ref.at[me], send.at[d], recv.at[d], ctx_id(to)).start()
-
-    for d in range(1, n_ctx):
-        to, came = me + sign * d, me - sign * d
-
-        @pl.when(inside(came))
+            remote(part, slots.at[me], send.at[d], recv.at[d], ctx_id(to)).start()
+
+    def arrive():
+        for d in range(1, 8):
+            came = me - sign * d
+
+            @pl.when(inside(came))
+            def _():
+                remote(part, slots.at[came], send.at[d], recv.at[d], ctx_id(came)).wait_recv()
+
+    def sent():
+        for d in range(1, 8):
+            to = me + sign * d
+
+            @pl.when(inside(to))
+            def _():
+                remote(part, slots.at[me], send.at[d], recv.at[d], ctx_id(to)).wait_send()
+
+    return arrive, sent
+
+
+def weigh(total, weight, slots, sign):
+    me = lax.axis_index("ctx")
+    total[...] = jnp.zeros_like(total)
+    for k in range(8):
+
+        @pl.when(k < me if sign > 0 else k > me)
         def _():
-            remote(part_ref, all_ref.at[came], send.at[d], recv.at[d], ctx_id(came)).wait_recv()
-
-        @pl.when(inside(to))
-        def _():
-            remote(part_ref, all_ref.at[me], send.at[d], recv.at[d], ctx_id(to)).wait_send()
-
-
-def spread_states(part, sign, number):
-    n_ctx = lax.axis_size("ctx")
-    if n_ctx != 8:
-        return lax.all_gather(part, "ctx", axis=0)
-    any_space = pl.BlockSpec(memory_space=pl.ANY)
-    return pl.pallas_call(
-        functools.partial(state_kernel, n_ctx, sign),
-        out_shape=jax.ShapeDtypeStruct((n_ctx,) + part.shape, part.dtype),
-        in_specs=[any_space],
-        out_specs=any_space,
-        scratch_shapes=[pltpu.SemaphoreType.DMA((n_ctx,)), pltpu.SemaphoreType.DMA((n_ctx,))],
-        compiler_params=pltpu.CompilerParams(collective_id=number, has_side_effects=True),
-        name="states_ahead" if sign > 0 else "states_back",
-    )(part)
+            total[...] += weight[k] * slots[k]
 
 
 def move_kernel(
-    cut, cot_ref, gated_ref, cots_ref, rows_ref, turned_ref, joined_ref,
+    cut, cot_ref, partial_ref, part_ref, near_ref, query_ref, ahead_ref, behind_ref, in_map_ref, out_map_ref,
+    cots_ref, rows_ref, turned_ref, joined_ref, signal_ref, query_grad_ref, returning_ref,
+    ahead_slots, back_slots, back_part, entering, filtered_ref, gated_ref, halves, arrived_halves, last_half,
+    ahead_send, ahead_recv, back_send, back_recv, half_sem, half_send, half_recv, last_send, last_recv,
     own_sem, f_recv, g_recv, q_recv, f_send, g_send, p_send, q_send,
     turn_send, turn_recv, join_send, join_recv, wide_send, wide_recv,
 ):
@@ -121,13 +124,74 @@
     y, core = ch // 2, ch % 2
     across = (1 - y) * 2 + core
     mate = y * 2 + 1 - core
+    far = (1 - y) * 2 + 1 - core
     length = cot_ref.shape[0]
     piece = turned_ref.shape[1]
+    group_rows = 4 * piece
     greet(
         [ctx_id(lax.rem(me + d, 8)) for d in range(1, 8)]
         + [ch_id(lax.rem(ch + d, 4)) for d in range(1, 4)]
     )
     first, rest = pl.ds(0, cut), pl.ds(cut, length - cut)
+    ahead_arrive, ahead_sent = state_copies(part_ref, ahead_slots, ahead_send, ahead_recv, 1)
+
+    to_mate = [
+        remote(partial_ref.at[index], arrived_halves.at[k], half_send.at[k], half_recv.at[k], ch_id(mate))
+        for k, index in ((0, far), (1, mate))
+    ]
+    own_halves = [
+        pltpu.make_async_copy(partial_ref.at[index], halves.at[k], half_sem.at[k])
+        for k, index in ((0, across), (1, ch))
+    ]
+    cot_copy = pltpu.make_async_copy(cot_ref, cots_ref.at[me], own_sem.at[2])
+
+    def to_twin_first():
+        return remote(cot_ref.at[first], cots_ref.at[me, first], p_send.at[0], g_recv.at[z], ctx_id(twin))
+
+    def to_twin_rest(origin, src):
+        slot = 2 * origin + x
+        return remote(src, cots_ref.at[slot, rest], q_send.at[origin], q_recv.at[origin], ctx_id(twin))
+
+    def along(origin, side, src):
+        slot = 2 * origin + x
+        to = me + 2 * side
+        return remote(src, cots_ref.at[slot], f_send.at[(side + 1) // 2, origin], f_recv.at[origin], ctx_id(to))
+
+    def along_first(origin, side):
+        slot = 2 * origin + 1 - x
+        to = me + 2 * side
+        part = cots_ref.at[slot, first]
+        return remote(part, part, g_send.at[(side + 1) // 2, origin], g_recv.at[origin], ctx_id(to))
+
+    def goes(side):
+        return z < 3 if side > 0 else z > 0
+
+    to_twin_first().start()
+    for side in (1, -1):
+
+        @pl.when(goes(side))
+        def _():
+            along(z, side, cot_ref).start()
+
+    to_twin_rest(z, cot_ref.at[rest]).start()
+    for copy in to_mate + own_halves + [cot_copy]:
+        copy.start()
+
+    ahead_arrive()
+    weigh(entering, ahead_ref, ahead_slots, 1)
+    for g in range(2):
+        carried = entering[g].T
+
+        for r in range(4):
+            rows = pl.ds(g * group_rows + r * piece, piece)
+            filtered = near_ref[rows, :] + jnp.dot(
+                carried[r * piece : (r + 1) * piece],
+                in_map_ref[g],
+                precision=lax.Precision.HIGHEST,
+                preferred_element_type=jnp.float32,
+            )
+            filtered_ref[rows, :] = filtered
+            gated_ref[g, r] = (query_ref[rows, :].astype(jnp.float32) * filtered).astype(jnp.bfloat16)
 
     turns = []
     for d in range(1, 4):
@@ -143,42 +207,24 @@
                 gated_ref.at[h, to], turned_ref.at[2 * came + h], turn_send.at[slot], turn_recv.at[slot], ch_id(to)
             )
             turns.append((out, back))
-    locals_ = [pltpu.make_async_copy(gated_ref.at[h, ch], turned_ref.at[2 * ch + h], own_sem.at[h]) for h in range(2)]
-    locals_.append(pltpu.make_async_copy(cot_ref, cots_ref.at[me], own_sem.at[2]))
-
-    def to_twin_first():
-        return remote(cot_ref.at[first], cots_ref.at[me, first], p_send.at[0], g_recv.at[z], ctx_id(twin))
-
-    def to_twin_rest(origin, src):
-        slot = 2 * origin + x
-        return remote(src, cots_ref.at[slot, rest], q_send.at[origin], q_recv.at[origin], ctx_id(twin))
-
-    def along(origin, side, src):
-        slot = 2 * origin + x
-        to = me + 2 * side
-        return remote(src, cots_ref.at[slot], f_send.at[(side + 1) // 2, origin], f_recv.at[origin], ctx_id(to))
-
-    def along_first(origin, side):
-        slot = 2 * origin + 1 - x
-        to = me + 2 * side
-        part = cots_ref.at[slot, first]
-        return remote(part, part, g_send.at[(side + 1) // 2, origin], g_recv.at[origin], ctx_id(to))
-
-    def goes(side):
-        return z < 3 if side > 0 else z > 0
-
-    to_twin_first().start()
-    for side in (1, -1):
-
-        @pl.when(goes(side))
-        def _():
-            along(z, side, cot_ref).start()
-
-    to_twin_rest(z, cot_ref.at[rest]).start()
-    for copy in locals_:
+    own_turns = [
+        pltpu.make_async_copy(gated_ref.at[h, ch], turned_ref.at[2 * ch + h], own_sem.at[h]) for h in range(2)
+    ]
+    for copy in own_turns:
         copy.start()
 
-    for copy in locals_[:2]:
+    own_halves[0].wait()
+    to_mate[0].wait_recv()
+
+    @pl.loop(0, 8)
+    def _(r):
+        rows = pl.ds(pl.multiple_of(r * piece, piece), piece)
+        halves[0, rows, :] += arrived_halves[0, rows, :]
+
+    to_across = remote(halves.at[0], last_half, last_send.at[0], last_recv.at[0], ch_id(across))
+    to_across.start()
+
+    for copy in own_turns:
         copy.wait()
     for out, back in turns:
         back.wait_recv()
@@ -253,10 +299,31 @@
     remote(joined_ref, rows_of(across), wide_send.at[0], wide_recv.at[0], ch_id(across)).wait_recv()
     wide_on = remote(rows_of(across), rows_of(across), wide_send.at[2], wide_recv.at[2], ch_id(mate))
     wide_on.start()
+    own_halves[1].wait()
+    to_mate[1].wait_recv()
+    to_across.wait_recv()
+    for g in range(2):
+
+        @pl.loop(0, 4)
+        def _(r):
+            rows = pl.ds(pl.multiple_of(g * group_rows + r * piece, piece), piece)
+            output_grad = halves[1, rows, :] + arrived_halves[1, rows, :] + last_half[rows, :]
+            signal_ref[rows, :] = output_grad * query_ref[rows, :].astype(jnp.float32)
+            query_grad_ref[rows, :] = (output_grad * filtered_ref[rows, :]).astype(jnp.bfloat16)
+
+        back_part[g] = lax.dot_general(
+            out_map_ref[g],
+            signal_ref[pl.ds(g * group_rows, group_rows), :],
+            (((1,), (1,)), ((), ())),
+            precision=lax.Precision.HIGHEST,
+            preferred_element_type=jnp.float32,
+        )
+    back_arrive, back_sent = state_copies(back_part, back_slots, back_send, back_recv, -1)
     step(3)
+    back_arrive()
+    weigh(returning_ref, behind_ref, back_slots, -1)
 
     remote(joined_ref, rows_of(mate), wide_send.at[1], wide_recv.at[1], ch_id(mate)).wait_recv()
-    far = (1 - y) * 2 + 1 - core
     remote(rows_of(across), rows_of(far), wide_send.at[2], wide_recv.at[2], ch_id(mate)).wait_recv()
     for origin in range(4):
         slot = 2 * origin + 1 - x
@@ -278,41 +345,74 @@
     wide_mate.wait_send()
     wide_on.wait_send()
     wide_own.wait()
-    locals_[2].wait()
-
-
-def move_all(gated, cotangent):
+    cot_copy.wait()
+    for copy in to_mate + [to_across]:
+        copy.wait_send()
+    ahead_sent()
+    back_sent()
+
+
+def move_all(cotangent, partial_grad, part, near, query, ahead, behind, in_map, out_map):
     n_ctx, n_ch = lax.axis_size("ctx"), lax.axis_size("ch")
-    rows, length = gated.shape
-    if (n_ctx, n_ch) != (8, 4) or rows % (2 * n_ch * 16) or length % 128:
-        return (
-            exchange_rows(gated, n_ctx, n_ch),
-            lax.all_gather(cotangent, "ctx", axis=0, tiled=True),
-        )
+    rows, length = query.shape
     piece = rows // 2 // n_ch
     width = cotangent.shape[1]
     any_space = pl.BlockSpec(memory_space=pl.ANY)
-    bf16 = jnp.bfloat16
+    vmem = pl.BlockSpec(memory_space=pltpu.VMEM)
+    f32, bf16 = jnp.float32, jnp.bfloat16
     dma = pltpu.SemaphoreType.DMA
-    cots, gathered, _, _ = pl.pallas_call(
+    cots, gathered, _, _, signal, query_grad, returning = pl.pallas_call(
         functools.partial(move_kernel, CUT),
         out_shape=(
             jax.ShapeDtypeStruct((n_ctx, length, width), bf16),
             jax.ShapeDtypeStruct((rows // 2, n_ctx * length), bf16),
             jax.ShapeDtypeStruct((n_ctx, piece, length), bf16),
             jax.ShapeDtypeStruct((piece, n_ctx * length), bf16),
+            jax.ShapeDtypeStruct((rows, length), f32),
+            jax.ShapeDtypeStruct((rows, length), bf16),
+            jax.ShapeDtypeStruct(part.shape, f32),
         ),
-        in_specs=[any_space] * 2,
-        out_specs=[any_space] * 4,
+        in_specs=[any_space, any_space] + [vmem] * 7,
+        out_specs=[any_space] * 4 + [vmem] * 3,
         scratch_shapes=[
+            pltpu.VMEM((n_ctx,) + part.shape, f32),
+            pltpu.VMEM((n_ctx,) + part.shape, f32),
+            pltpu.VMEM(part.shape, f32),
+            pltpu.VMEM(part.shape, f32),
+            pltpu.VMEM((rows, length), f32),
+            pltpu.VMEM((2, n_ch, piece, length), bf16),
+            pltpu.VMEM((2, rows, length), f32),
+            pltpu.VMEM((2, rows, length), f32),
+            pltpu.VMEM((rows, length), f32),
+            dma((8,)), dma((8,)), dma((8,)), dma((8,)), dma((2,)), dma((2,)), dma((2,)), dma((1,)), dma((1,)),
             dma((5,)), dma((4,)), dma((4,)), dma((4,)), dma((2, 4)), dma((2, 4)), dma((1,)), dma((4,)),
             dma((8,)), dma((8,)), dma((8,)), dma((8,)), dma((3,)), dma((3,)),
         ],
-        compiler_params=pltpu.CompilerParams(collective_id=2, has_side_effects=True),
+        compiler_params=pltpu.CompilerParams(
+            collective_id=0, has_side_effects=True, vmem_limit_bytes=48 * 1024 * 1024
+        ),
         cost_estimate=pl.CostEstimate(flops=0, bytes_accessed=300_000_000, transcendentals=0),
         name="move_all",
-    )(cotangent, gated.reshape(2, n_ch, piece, length))
-    return gathered, cots.reshape(n_ctx * length, width)
+    )(cotangent, partial_grad.reshape(n_ch, rows, length), part, near, query, ahead, behind, in_map, out_map)
+    return signal, query_grad, returning, gathered, cots.reshape(n_ctx * length, width)
+
+
+def move_by_collectives(cotangent, partial_grad, part, near, query, ahead, behind, in_map, out_map):
+    n_ctx, n_ch = lax.axis_size("ctx"), lax.axis_size("ch")
+    groups = part.shape[0]
+    rows, length = query.shape
+    query_f = query.astype(jnp.float32)
+    cots = lax.all_gather(cotangent, "ctx", axis=0, tiled=True)
+    output_grad = lax.psum_scatter(partial_grad, "ch", scatter_dimension=0, tiled=True)
+    entering = jnp.sum(ahead * lax.all_gather(part, "ctx", axis=0), axis=0)
+    carried = jnp.einsum("gnc,gnt->gct", entering, in_map, precision=HIGH).reshape(rows, length)
+    filtered = near + carried
+    gathered = exchange_rows((query_f * filtered).astype(jnp.bfloat16), n_ctx, n_ch)
+    signal = output_grad * query_f
+    back_part = jnp.einsum("gnl,gcl->gnc", out_map, signal.reshape(groups, rows // groups, length), precision=HIGH)
+    returning = jnp.sum(behind * lax.all_gather(back_part, "ctx", axis=0), axis=0)
+    query_grad = (output_grad * filtered).astype(jnp.bfloat16)
+    return signal, query_grad, returning, gathered, cots
 
 
 def local(
@@ -356,35 +456,30 @@
 
     key_f = key_input.astype(jnp.float32)
     value_f = value_input.astype(jnp.float32)
-    query_f = query_input.astype(jnp.float32)
     mixed = (key_f * value_f).reshape(groups, group_rows, length)
     forward_part = jnp.einsum("gnl,gcl->gnc", carry_out_map, mixed, precision=HIGH)
-    forward_all = spread_states(forward_part, 1, 0)
-    entering = jnp.sum(
-        jnp.where(joined_ahead[:, None, None, None], ahead_weight[..., None] * forward_all, 0.0), axis=0
-    )
-
     partial_grad = lax.dot_general(
         out_weight, out_cotangent, (((1,), (1,)), ((), ())), preferred_element_type=jnp.float32
     )
-    output_grad = lax.psum_scatter(partial_grad, "ch", scatter_dimension=0, tiled=True)
 
     kernel = local_kernel(decay_rate, residue, doc_ids, length)
-    filtered = jnp.einsum("gcs,gts->gct", mixed, kernel, precision=HIGH)
-    filtered = filtered + jnp.einsum("gnc,gnt->gct", entering, carry_in_map, precision=HIGH)
-    filtered = filtered.reshape(rows_here, length)
-    gated = (query_f * filtered).astype(jnp.bfloat16)
-    gated_rows, cotangent_all = move_all(gated, out_cotangent)
-    output_grad, gated_rows, cotangent_all = lax.optimization_barrier((output_grad, gated_rows, cotangent_all))
-
-    signal = (output_grad * query_f).reshape(groups, group_rows, length)
-    backward_part = jnp.einsum("gnl,gcl->gnc", back_out_map, signal, precision=HIGH)
-    backward_all = spread_states(backward_part, -1, 1)
-    query_grad = (output_grad * filtered).astype(jnp.bfloat16)
+    near = jnp.einsum("gcs,gts->gct", mixed, kernel, precision=HIGH).reshape(rows_here, length)
+    wide = (n_ctx,) + forward_part.shape
+    on_kernel = (n_ctx, n_ch, groups) == (8, 4, 2) and rows_here == 1024 and length == 512
+    move = move_all if on_kernel else move_by_collectives
+    signal, query_grad, returning, gated_rows, cotangent_all = move(
+        out_cotangent,
+        partial_grad,
+        forward_part,
+        near,
+        query_input,
+        jnp.broadcast_to(ahead_weight[..., None], wide),
+        jnp.broadcast_to(back_weight[..., None], wide),
+        carry_in_map,
+        back_out_map,
+    )
+    signal = signal.reshape(groups, group_rows, length)
     spread = jnp.einsum("gct,gts->gcs", signal, kernel, precision=HIGH)
-    returning = jnp.sum(
-        jnp.where(joined_back[:, None, None, None], back_weight[..., None] * backward_all, 0.0), axis=0
-    )
     spread = spread + jnp.einsum("gnc,gns->gcs", returning, back_in_map, precision=HIGH)
     spread = spread.reshape(rows_here, length)
     key_grad = (spread * value_f).astype(jnp.bfloat16)

time: 220 us -> 170 us (0.77)
  the two profiles are of different devices: /device:TPU:4 before, /device:TPU:24 now
where the time goes in v3:
time: 170 us
  Pallas kernels  132 us (78%)
  matrix products  26.5 us (16%)
  other arithmetic  7.77 us (5%)
  local copies, waits for them, and re-layouts  1.86 us (1%)
    pallas_call x1, Pallas kernels, move_all(): pl.pallas_call(functools.partial(move_kernel, CUT), out_shape=(jax.ShapeD...  132 us
    dot_general x1, matrix products, local(): jnp.dot(gated_rows, cotangent_all, preferred_element_type=jnp.float32)  10.6 us
    dot_general x1, matrix products, local(): lax.dot_general(out_weight, out_cotangent, (((1,), (1,)), ((), ())), pref...  7.41 us

profile of v3, /device:TPU:24, one launch (start us, length us, event | category | flops | bytes accessed | tf_op | source)
XLA Modules:
  0.0 169.5 jit_solution(8515502309013785223)
XLA Ops:
  0.7 1.4 fusion.39
  2.8 0.7 convert_reduce_fusion
  3.5 0.6 slice.15
  4.1 0.7 convert_reduce_fusion.1
  4.8 0.7 compare_and_fusion
  5.6 0.7 neg.5
  6.2 0.1 exponential_select_fusion
  6.4 0.1 broadcast_in_dim.34.ahead_ref
  6.5 0.1 broadcast_in_dim.36.behind_ref
  6.6 1.4 fusion.14
  8.1 0.2 fusion.5
  8.3 0.3 convert_multiply_fusion.1
  8.6 0.0 slice-start.1
  8.7 3.2 %fusion.8 = f32[2,512,512]{2,1,0:T(8,128)} fusion(f32[2,512,512]{2,1,0:T(8,128)S(1)} %bitcast.19, f32[2,128,128]{1,2,0:T(8,128)S(1)} %slice.22, f32[2,256,128]{1,2,0:T(8,128)S(1)} %slice.21, f32[2,384,128]{1,2,0:T(8,128)S(1)} %slice.20, f32[2,512,128]{1,2,0:T(8,128)S(1)} %fusion.14, pred[512,512]{0,1:T(8,128)(4,1)S(1)} %fusion.5), kind=kOutput, calls=%fused_computation.21 | convolution fusion | flops 1617952768 | bytes 5767168 | tf_op jit(solution)/shard_map/gcs,gts->gct/dot_general | solution.py:466
  11.9 0.7 compare_convert_fusion
  12.6 1.0 fusion.18.part_ref
  13.7 0.1 exponential_multiply_fusion
  13.8 7.4 %fusion.50 = f32[4096,512]{1,0:T(8,128)} fusion(bf16[4096,1024]{1,0:T(8,128)(2,1)S(1)} %bitcast.24, bf16[512,1024]{1,0:T(8,128)(2,1)S(1)} %copy-done), kind=kOutput, calls=%fused_computation.82 | convolution fusion | flops 4294967296 | bytes 17825792 | tf_op jit(solution)/shard_map/dot_general | solution.py:461
  21.2 131.8 %move_all.1 = (bf16[8,512,1024]{2,1,0:T(8,128)(2,1)}, bf16[512,4096]{1,0:T(8,128)(2,1)}, bf16[8,128,512]{2,1,0:T(8,128)(2,1)}, bf16[128,4096]{1,0:T(8,128)(2,1)}...) custom-call(bf16[512,1024]{1,0:T(8,128)(2,1)S(1)} %copy-done, ...), custom_call_target="tpu_custom_call" | custom-call | bytes 300000000 | tf_op jit(solution)/shard_map/move_all/pallas_call | solution.py:364
  153.1 10.6 %convolution_multiply_fusion = f32[512,1024]{1,0:T(8,128)} fusion(bf16[512,4096]{1,0:T(8,128)(2,1)} %get-tuple-element.12, bf16[4096,1024]{1,0:T(8,128)(2,1)} %bitcast.25), kind=kOutput, calls=%fused_computation.17 | convolution fusion | flops 4295491584 | bytes 14680064 | tf_op jit(solution)/shard_map/dot_general | solution.py:489
  163.7 1.9 %fusion.6 = f32[2,512,512]{2,1,0:T(8,128)S(1)} fusion(f32[2,512,512]{2,1,0:T(8,128)S(1)} %bitcast.26, f32[2,128,128]{1,2,0:T(8,128)S(1)} %slice.22, f32[2,256,128]{1,2,0:T(8,128)S(1)} %slice.21, f32[2,384,128]{1,2,0:T(8,128)S(1)} %slice.20, f32[2,512,128]{1,2,0:T(8,128)S(1)} %fusion.14, pred[512,512]{0,1:T(8,128)(4,1)S(1)} %fusion.5), kind=kOutput, calls=%fused_computation.20 | convolution fusion | flops 1617952768 | bytes 5767168 | tf_op jit(solution)/shard_map/gct,gts->gcs/dot_general | solution.py:482
  165.6 1.0 convolution_add_fusion
  166.6 1.9 %fusion = (bf16[1024,512]{1,0:T(8,128)(2,1)}, bf16[1024,512]{1,0:T(8,128)(2,1)}) fusion(bf16[1024,512]{1,0:T(8,128)(2,1)S(1)} %copy-done.2, f32[2,512,512]{2,1,0:T(8,128)S(1)} %convolution_add_fusion, bf16[1024,512]{1,0:T(8,128)(2,1)S(1)} %copy-done.1), kind=kLoop, calls=%fused_computation.7 | loop fusion | flops 3145728 | bytes 6291456 | tf_op jit(solution)/shard_map/convert_element_type | solution.py:486
  168.5 1.0 copy.19
  (26 shorter events, 0.2 us)
Async XLA Ops:
  0.6 7.7 %copy-start.1 = (bf16[1024,512]{1,0:T(8,128)(2,1)S(1)}, bf16[1024,512]{1,0:T(8,128)(2,1)}, u32[]{:S(2)}) copy-start(bf16[1024,512]{1,0:T(8,128)(2,1)} %param.10) | copy-start | bytes 3145732
  0.6 7.7 %copy-start.2 = (bf16[1024,512]{1,0:T(8,128)(2,1)S(1)}, bf16[1024,512]{1,0:T(8,128)(2,1)}, u32[]{:S(2)}) copy-start(bf16[1024,512]{1,0:T(8,128)(2,1)} %param.9) | copy-start | bytes 3145732
  8.3 5.4 %slice-start = ((s8[8388608]{0:T(1024)(128)(4,1)}), s8[4194304]{0:T(1024)(128)(4,1)S(1)}, s32[]{:S(2)}) async-start(s8[8388608]{0:T(1024)(128)(4,1)} %bitcast.23), calls=%async_computation | async-start | bytes 8388608
  8.6 5.1 %slice-start.1 = ((s8[8388608]{0:T(1024)(128)(4,1)}), s8[4194304]{0:T(1024)(128)(4,1)S(1)}, s32[]{:S(2)}) async-start(s8[8388608]{0:T(1024)(128)(4,1)} %bitcast.23), calls=%async_computation.1 | async-start | bytes 8388608
  11.9 1.8 %copy-start.3 = (f32[2,16]{1,0:T(2,128)S(1)}, f32[2,16]{1,0:T(2,128)}, u32[]{:S(2)}) copy-start(f32[2,16]{1,0:T(2,128)} %param.12) | copy-start | bytes 388
  11.9 1.9 %copy-start = (bf16[512,1024]{1,0:T(8,128)(2,1)S(1)}, bf16[512,1024]{1,0:T(8,128)(2,1)}, u32[]{:S(2)}) copy-start(bf16[512,1024]{1,0:T(8,128)(2,1)} %cot_ref.1) | copy-start | bytes 3145732
  153.1 10.6 %copy-start.4 = (f32[1024,512]{1,0:T(8,128)S(1)}, f32[1024,512]{1,0:T(8,128)}, u32[]{:S(2)}) copy-start(f32[1024,512]{1,0:T(8,128)} %get-tuple-element.10) | copy-start | bytes 6291460

commit v4 on v3

--- a/solution.py
+++ b/solution.py
@@ -111,9 +111,9 @@
 
 
 def move_kernel(
-    cut, cot_ref, partial_ref, part_ref, near_ref, query_ref, ahead_ref, behind_ref, in_map_ref, out_map_ref,
+    cut, cot_ref, weight_ref, cot_near, part_ref, near_ref, query_ref, ahead_ref, behind_ref, in_map_ref, out_map_ref,
     cots_ref, rows_ref, turned_ref, joined_ref, signal_ref, query_grad_ref, returning_ref,
-    ahead_slots, back_slots, back_part, entering, filtered_ref, gated_ref, halves, arrived_halves, last_half,
+    ahead_slots, back_slots, back_part, entering, filtered_ref, gated_ref, weights, partial_ref, arrived_halves, last_half,
     ahead_send, ahead_recv, back_send, back_recv, half_sem, half_send, half_recv, last_send, last_recv,
     own_sem, f_recv, g_recv, q_recv, f_send, g_send, p_send, q_send,
     turn_send, turn_recv, join_send, join_recv, wide_send, wide_recv,
@@ -132,30 +132,54 @@
         [ctx_id(lax.rem(me + d, 8)) for d in range(1, 8)]
         + [ch_id(lax.rem(ch + d, 4)) for d in range(1, 4)]
     )
-    first, rest = pl.ds(0, cut), pl.ds(cut, length - cut)
+    first = pl.ds(0, cut)
     ahead_arrive, ahead_sent = state_copies(part_ref, ahead_slots, ahead_send, ahead_recv, 1)
 
     to_mate = [
         remote(partial_ref.at[index], arrived_halves.at[k], half_send.at[k], half_recv.at[k], ch_id(mate))
         for k, index in ((0, far), (1, mate))
     ]
-    own_halves = [
-        pltpu.make_async_copy(partial_ref.at[index], halves.at[k], half_sem.at[k])
-        for k, index in ((0, across), (1, ch))
+    rows_here = last_half.shape[0]
+    load_weights = [
+        pltpu.make_async_copy(
+            weight_ref.at[pl.ds(pl.multiple_of(index * rows_here, rows_here), rows_here)],
+            weights.at[k],
+            half_sem.at[k],
+        )
+        for k, index in enumerate((far, across, mate, ch))
     ]
+
+    def multiply(k, index):
+        load_weights[k].wait()
+
+        @pl.loop(0, 4)
+        def _(r):
+            rows = pl.ds(pl.multiple_of(r * 2 * piece, piece), 2 * piece)
+            partial_ref[index, rows, :] = lax.dot_general(
+                weights[k, rows, :], cot_near[...], (((1,), (1,)), ((), ())), preferred_element_type=jnp.float32
+            )
+
     cot_copy = pltpu.make_async_copy(cot_ref, cots_ref.at[me], own_sem.at[2])
 
     def to_twin_first():
         return remote(cot_ref.at[first], cots_ref.at[me, first], p_send.at[0], g_recv.at[z], ctx_id(twin))
 
-    def to_twin_rest(origin, src):
-        slot = 2 * origin + x
-        return remote(src, cots_ref.at[slot, rest], q_send.at[origin], q_recv.at[origin], ctx_id(twin))
-
-    def along(origin, side, src):
-        slot = 2 * origin + x
-        to = me + 2 * side
-        return remote(src, cots_ref.at[slot], f_send.at[(side + 1) // 2, origin], f_recv.at[origin], ctx_id(to))
+    half = length // 2
+    along_rows = (pl.ds(0, half), pl.ds(half, half))
+    rest_rows = (pl.ds(cut, half - cut), pl.ds(half, half))
+
+    def to_twin_rest(origin, part, src=None):
+        rows = rest_rows[part]
+        to = cots_ref.at[2 * origin + x, rows]
+        src = to if src is None else src.at[rows]
+        return remote(src, to, q_send.at[part, origin], q_recv.at[part, origin], ctx_id(twin))
+
+    def along(origin, side, part, src=None):
+        rows = along_rows[part]
+        to = cots_ref.at[2 * origin + x, rows]
+        src = to if src is None else src.at[rows]
+        way = (side + 1) // 2
+        return remote(src, to, f_send.at[way, part, origin], f_recv.at[part, origin], ctx_id(me + 2 * side))
 
     def along_first(origin, side):
         slot = 2 * origin + 1 - x
@@ -171,11 +195,15 @@
 
         @pl.when(goes(side))
         def _():
-            along(z, side, cot_ref).start()
-
-    to_twin_rest(z, cot_ref.at[rest]).start()
-    for copy in to_mate + own_halves + [cot_copy]:
+            for part in range(2):
+                along(z, side, part, cot_ref).start()
+
+    for part in range(2):
+        to_twin_rest(z, part, cot_ref).start()
+    for copy in load_weights + [cot_copy]:
         copy.start()
+    multiply(0, far)
+    to_mate[0].start()
 
     ahead_arrive()
     weigh(entering, ahead_ref, ahead_slots, 1)
@@ -213,16 +241,18 @@
     for copy in own_turns:
         copy.start()
 
-    own_halves[0].wait()
+    multiply(1, across)
     to_mate[0].wait_recv()
 
     @pl.loop(0, 8)
     def _(r):
         rows = pl.ds(pl.multiple_of(r * piece, piece), piece)
-        halves[0, rows, :] += arrived_halves[0, rows, :]
-
-    to_across = remote(halves.at[0], last_half, last_send.at[0], last_recv.at[0], ch_id(across))
+        partial_ref[across, rows, :] += arrived_halves[0, rows, :]
+
+    to_across = remote(partial_ref.at[across], last_half, last_send.at[0], last_recv.at[0], ch_id(across))
     to_across.start()
+    multiply(2, mate)
+    to_mate[1].start()
 
     for copy in own_turns:
         copy.wait()
@@ -254,21 +284,22 @@
         def _():
             along_first(z, side).start()
 
+    multiply(3, ch)
+
     def step(s):
         for side in (1, -1):
             origin = z - side * s
 
             @pl.when((origin >= 0) & (origin <= 3))
             def _():
-                slot = 2 * origin + x
-                arrived = cots_ref.at[slot]
-                along(origin, side, arrived).wait_recv()
-
-                @pl.when(goes(side))
-                def _():
-                    along(origin, side, arrived).start()
-
-                to_twin_rest(origin, cots_ref.at[slot, rest]).start()
+                for part in range(2):
+                    along(origin, side, part).wait_recv()
+
+                    @pl.when(goes(side))
+                    def _():
+                        along(origin, side, part).start()
+
+                    to_twin_rest(origin, part).start()
 
         for side in (1, -1):
             origin = z - side * s
@@ -299,7 +330,6 @@
     remote(joined_ref, rows_of(across), wide_send.at[0], wide_recv.at[0], ch_id(across)).wait_recv()
     wide_on = remote(rows_of(across), rows_of(across), wide_send.at[2], wide_recv.at[2], ch_id(mate))
     wide_on.start()
-    own_halves[1].wait()
     to_mate[1].wait_recv()
     to_across.wait_recv()
     for g in range(2):
@@ -307,7 +337,7 @@
         @pl.loop(0, 4)
         def _(r):
             rows = pl.ds(pl.multiple_of(g * group_rows + r * piece, piece), piece)
-            output_grad = halves[1, rows, :] + arrived_halves[1, rows, :] + last_half[rows, :]
+            output_grad = partial_ref[ch, rows, :] + arrived_halves[1, rows, :] + last_half[rows, :]
             signal_ref[rows, :] = output_grad * query_ref[rows, :].astype(jnp.float32)
             query_grad_ref[rows, :] = (output_grad * filtered_ref[rows, :]).astype(jnp.bfloat16)
 
@@ -326,17 +356,19 @@
     remote(joined_ref, rows_of(mate), wide_send.at[1], wide_recv.at[1], ch_id(mate)).wait_recv()
     remote(rows_of(across), rows_of(far), wide_send.at[2], wide_recv.at[2], ch_id(mate)).wait_recv()
     for origin in range(4):
-        slot = 2 * origin + 1 - x
-        part = cots_ref.at[slot, rest]
-        remote(part, part, q_send.at[origin], q_recv.at[origin], ctx_id(twin)).wait_recv()
+        for part in range(2):
+            block = cots_ref.at[2 * origin + 1 - x, rest_rows[part]]
+            remote(block, block, q_send.at[part, origin], q_recv.at[part, origin], ctx_id(twin)).wait_recv()
     to_twin_first().wait_send()
     for origin in range(4):
-        to_twin_rest(origin, cot_ref.at[rest]).wait_send()
+        for part in range(2):
+            to_twin_rest(origin, part).wait_send()
         for side in (1, -1):
 
             @pl.when(goes(side) & (origin <= z if side > 0 else origin >= z))
             def _():
-                along(origin, side, cot_ref).wait_send()
+                for part in range(2):
+                    along(origin, side, part).wait_send()
                 along_first(origin, side).wait_send()
 
     for out, back in turns + joins:
@@ -352,7 +384,7 @@
     back_sent()
 
 
-def move_all(cotangent, partial_grad, part, near, query, ahead, behind, in_map, out_map):
+def move_all(cotangent, weight, part, near, query, ahead, behind, in_map, out_map):
     n_ctx, n_ch = lax.axis_size("ctx"), lax.axis_size("ch")
     rows, length = query.shape
     piece = rows // 2 // n_ch
@@ -372,7 +404,7 @@
             jax.ShapeDtypeStruct((rows, length), bf16),
             jax.ShapeDtypeStruct(part.shape, f32),
         ),
-        in_specs=[any_space, any_space] + [vmem] * 7,
+        in_specs=[any_space, any_space] + [vmem] * 8,
         out_specs=[any_space] * 4 + [vmem] * 3,
         scratch_shapes=[
             pltpu.VMEM((n_ctx,) + part.shape, f32),
@@ -381,28 +413,32 @@
             pltpu.VMEM(part.shape, f32),
             pltpu.VMEM((rows, length), f32),
             pltpu.VMEM((2, n_ch, piece, length), bf16),
-            pltpu.VMEM((2, rows, length), f32),
+            pltpu.VMEM((n_ch, rows, width), bf16),
+            pltpu.VMEM((n_ch, rows, length), f32),
             pltpu.VMEM((2, rows, length), f32),
             pltpu.VMEM((rows, length), f32),
-            dma((8,)), dma((8,)), dma((8,)), dma((8,)), dma((2,)), dma((2,)), dma((2,)), dma((1,)), dma((1,)),
-            dma((5,)), dma((4,)), dma((4,)), dma((4,)), dma((2, 4)), dma((2, 4)), dma((1,)), dma((4,)),
+            dma((8,)), dma((8,)), dma((8,)), dma((8,)), dma((4,)), dma((2,)), dma((2,)), dma((1,)), dma((1,)),
+            dma((5,)), dma((2, 4)), dma((4,)), dma((2, 4)), dma((2, 2, 4)), dma((2, 4)), dma((1,)), dma((2, 4)),
             dma((8,)), dma((8,)), dma((8,)), dma((8,)), dma((3,)), dma((3,)),
         ],
         compiler_params=pltpu.CompilerParams(
-            collective_id=0, has_side_effects=True, vmem_limit_bytes=48 * 1024 * 1024
+            collective_id=0, has_side_effects=True, vmem_limit_bytes=52 * 1024 * 1024
         ),
         cost_estimate=pl.CostEstimate(flops=0, bytes_accessed=300_000_000, transcendentals=0),
         name="move_all",
-    )(cotangent, partial_grad.reshape(n_ch, rows, length), part, near, query, ahead, behind, in_map, out_map)
+    )(cotangent, weight, cotangent, part, near, query, ahead, behind, in_map, out_map)
     return signal, query_grad, returning, gathered, cots.reshape(n_ctx * length, width)
 
 
-def move_by_collectives(cotangent, partial_grad, part, near, query, ahead, behind, in_map, out_map):
+def move_by_collectives(cotangent, weight, part, near, query, ahead, behind, in_map, out_map):
     n_ctx, n_ch = lax.axis_size("ctx"), lax.axis_size("ch")
     groups = part.shape[0]
     rows, length = query.shape
     query_f = query.astype(jnp.float32)
     cots = lax.all_gather(cotangent, "ctx", axis=0, tiled=True)
+    partial_grad = lax.dot_general(
+        weight, cotangent, (((1,), (1,)), ((), ())), preferred_element_type=jnp.float32
+    )
     output_grad = lax.psum_scatter(partial_grad, "ch", scatter_dimension=0, tiled=True)
     entering = jnp.sum(ahead * lax.all_gather(part, "ctx", axis=0), axis=0)
     carried = jnp.einsum("gnc,gnt->gct", entering, in_map, precision=HIGH).reshape(rows, length)
@@ -458,10 +494,6 @@
     value_f = value_input.astype(jnp.float32)
     mixed = (key_f * value_f).reshape(groups, group_rows, length)
     forward_part = jnp.einsum("gnl,gcl->gnc", carry_out_map, mixed, precision=HIGH)
-    partial_grad = lax.dot_general(
-        out_weight, out_cotangent, (((1,), (1,)), ((), ())), preferred_element_type=jnp.float32
-    )
-
     kernel = local_kernel(decay_rate, residue, doc_ids, length)
     near = jnp.einsum("gcs,gts->gct", mixed, kernel, precision=HIGH).reshape(rows_here, length)
     wide = (n_ctx,) + forward_part.shape
@@ -469,7 +501,7 @@
     move = move_all if on_kernel else move_by_collectives
     signal, query_grad, returning, gated_rows, cotangent_all = move(
         out_cotangent,
-        partial_grad,
+        out_weight,
         forward_part,
         near,
         query_input,

time: 170 us -> 154 us (0.906)
  Pallas kernels: 132 us -> 124 us
  matrix products: 26.5 us -> 19.1 us
    pallas_call x1, Pallas kernels: 132 us -> 124 us  [move_all(): pl.pallas_call(functools.partial(move_kernel, CUT), out_shape=(jax.ShapeD...]
    dot_general x1 -> x0, matrix products: 7.41 us -> none  [local(): lax.dot_general(out_weight, out_cotangent, (((1,), (1,)), ((), ())), pref...]
where the time goes in v4:
time: 154 us
  Pallas kernels  124 us (81%)
  matrix products  19.1 us (12%)
  other arithmetic  7.68 us (5%)
  local copies, waits for them, and re-layouts  1.85 us (1%)
    pallas_call x1, Pallas kernels, move_all(): pl.pallas_call(functools.partial(move_kernel, CUT), out_shape=(jax.ShapeD...  124 us
    dot_general x1, matrix products, local(): jnp.dot(gated_rows, cotangent_all, preferred_element_type=jnp.float32)  10.6 us
    dot_general x1, matrix products, local(): jnp.einsum('gcs,gts->gct', mixed, kernel, precision=HIGH)  3.22 us

profile of v4, /device:TPU:24, one launch (start us, length us, event | category | flops | bytes accessed | tf_op | source)
XLA Modules:
  0.0 153.7 jit_solution(13314705195367511708)
XLA Ops:
  0.7 1.4 fusion.39
  2.8 0.7 convert_reduce_fusion
  3.5 0.6 slice.15
  4.1 0.7 convert_reduce_fusion.1
  4.8 0.7 compare_and_fusion
  5.6 0.7 neg.5
  6.2 0.1 exponential_select_fusion
  6.4 0.1 broadcast_in_dim.34.ahead_ref
  6.5 0.1 broadcast_in_dim.36.behind_ref
  6.6 1.4 fusion.14
  8.1 0.2 fusion.5
  8.3 0.3 convert_multiply_fusion.1
  8.6 3.2 %fusion.8 = f32[2,512,512]{2,1,0:T(8,128)} fusion(f32[2,512,512]{2,1,0:T(8,128)S(1)} %bitcast.15, f32[2,128,128]{1,2,0:T(8,128)S(1)} %slice.22, f32[2,256,128]{1,2,0:T(8,128)S(1)} %slice.21, f32[2,384,128]{1,2,0:T(8,128)S(1)} %slice.20, f32[2,512,128]{1,2,0:T(8,128)S(1)} %fusion.14, pred[512,512]{0,1:T(8,128)(4,1)S(1)} %fusion.5), kind=kOutput, calls=%fused_computation.21 | convolution fusion | flops 1617952768 | bytes 5767168 | tf_op jit(solution)/shard_map/gcs,gts->gct/dot_general | solution.py:498
  11.8 0.7 compare_convert_fusion
  12.5 1.0 fusion.18.part_ref
  13.6 0.1 exponential_multiply_fusion
  13.7 123.5 %move_all.1 = (bf16[8,512,1024]{2,1,0:T(8,128)(2,1)}, bf16[512,4096]{1,0:T(8,128)(2,1)}, bf16[8,128,512]{2,1,0:T(8,128)(2,1)}, bf16[128,4096]{1,0:T(8,128)(2,1)}...) custom-call(bf16[512,1024]{1,0:T(8,128)(2,1)} %cot_near.1, ...), custom_call_target="tpu_custom_call" | custom-call | bytes 300000000 | tf_op jit(solution)/shard_map/move_all/pallas_call | solution.py:396
  137.2 0.0 copy-start.4
  137.2 10.6 %convolution_multiply_fusion = f32[512,1024]{1,0:T(8,128)} fusion(bf16[512,4096]{1,0:T(8,128)(2,1)} %get-tuple-element.12, bf16[4096,1024]{1,0:T(8,128)(2,1)} %bitcast.19), kind=kOutput, calls=%fused_computation.17 | convolution fusion | flops 4295491584 | bytes 14680064 | tf_op jit(solution)/shard_map/dot_general | solution.py:521
  147.8 1.9 %fusion.6 = f32[2,512,512]{2,1,0:T(8,128)S(1)} fusion(f32[2,512,512]{2,1,0:T(8,128)S(1)} %bitcast.20, f32[2,128,128]{1,2,0:T(8,128)S(1)} %slice.22, f32[2,256,128]{1,2,0:T(8,128)S(1)} %slice.21, f32[2,384,128]{1,2,0:T(8,128)S(1)} %slice.20, f32[2,512,128]{1,2,0:T(8,128)S(1)} %fusion.14, pred[512,512]{0,1:T(8,128)(4,1)S(1)} %fusion.5), kind=kOutput, calls=%fused_computation.20 | convolution fusion | flops 1617952768 | bytes 5767168 | tf_op jit(solution)/shard_map/gct,gts->gcs/dot_general | solution.py:514
  149.7 1.0 convolution_add_fusion
  150.8 1.9 %fusion = (bf16[1024,512]{1,0:T(8,128)(2,1)}, bf16[1024,512]{1,0:T(8,128)(2,1)}) fusion(bf16[1024,512]{1,0:T(8,128)(2,1)S(1)} %copy-done.1, f32[2,512,512]{2,1,0:T(8,128)S(1)} %convolution_add_fusion, bf16[1024,512]{1,0:T(8,128)(2,1)S(1)} %copy-done), kind=kLoop, calls=%fused_computation.7 | loop fusion | flops 3145728 | bytes 6291456 | tf_op jit(solution)/shard_map/convert_element_type | solution.py:518
  152.7 0.0 copy-done.2
  152.7 1.0 copy.19
  (20 shorter events, 0.1 us)
Async XLA Ops:
  0.6 7.7 %copy-start = (bf16[1024,512]{1,0:T(8,128)(2,1)S(1)}, bf16[1024,512]{1,0:T(8,128)(2,1)}, u32[]{:S(2)}) copy-start(bf16[1024,512]{1,0:T(8,128)(2,1)} %param.10) | copy-start | bytes 3145732
  0.6 7.7 %copy-start.1 = (bf16[1024,512]{1,0:T(8,128)(2,1)S(1)}, bf16[1024,512]{1,0:T(8,128)(2,1)}, u32[]{:S(2)}) copy-start(bf16[1024,512]{1,0:T(8,128)(2,1)} %param.9) | copy-start | bytes 3145732
  11.8 1.7 %copy-start.3 = (f32[2,16]{1,0:T(2,128)S(1)}, f32[2,16]{1,0:T(2,128)}, u32[]{:S(2)}) copy-start(f32[2,16]{1,0:T(2,128)} %param.12) | copy-start | bytes 388
  137.2 10.6 %copy-start.4 = (f32[1024,512]{1,0:T(8,128)S(1)}, f32[1024,512]{1,0:T(8,128)}, u32[]{:S(2)}) copy-start(f32[1024,512]{1,0:T(8,128)} %get-tuple-element.10) | copy-start | bytes 6291460
  150.8 1.9 %copy-start.2 = (bf16[1024,512]{1,0:T(8,128)(2,1)S(1)}, bf16[1024,512]{1,0:T(8,128)(2,1)}, u32[]{:S(2)}) copy-start(bf16[1024,512]{1,0:T(8,128)(2,1)} %get-tuple-element.30) | copy-start | bytes 3145732

commit v5 on v4

--- a/solution.py
+++ b/solution.py
@@ -11,7 +11,8 @@
 MESH = pl.DeviceIdType.MESH
 HIGH = lax.Precision.HIGH
 TILE = 128
-CUT = 96
+CUT = 16
+PARTS = 4
 
 
 def doc_of(doc_ends, positions):
@@ -164,9 +165,9 @@
     def to_twin_first():
         return remote(cot_ref.at[first], cots_ref.at[me, first], p_send.at[0], g_recv.at[z], ctx_id(twin))
 
-    half = length // 2
-    along_rows = (pl.ds(0, half), pl.ds(half, half))
-    rest_rows = (pl.ds(cut, half - cut), pl.ds(half, half))
+    share = length // PARTS
+    along_rows = [pl.ds(part * share, share) for part in range(PARTS)]
+    rest_rows = [pl.ds(cut, share - cut)] + along_rows[1:]
 
     def to_twin_rest(origin, part, src=None):
         rows = rest_rows[part]
@@ -195,10 +196,10 @@
 
         @pl.when(goes(side))
         def _():
-            for part in range(2):
+            for part in range(PARTS):
                 along(z, side, part, cot_ref).start()
 
-    for part in range(2):
+    for part in range(PARTS):
         to_twin_rest(z, part, cot_ref).start()
     for copy in load_weights + [cot_copy]:
         copy.start()
@@ -292,7 +293,7 @@
 
             @pl.when((origin >= 0) & (origin <= 3))
             def _():
-                for part in range(2):
+                for part in range(PARTS):
                     along(origin, side, part).wait_recv()
 
                     @pl.when(goes(side))
@@ -356,18 +357,18 @@
     remote(joined_ref, rows_of(mate), wide_send.at[1], wide_recv.at[1], ch_id(mate)).wait_recv()
     remote(rows_of(across), rows_of(far), wide_send.at[2], wide_recv.at[2], ch_id(mate)).wait_recv()
     for origin in range(4):
-        for part in range(2):
+        for part in range(PARTS):
             block = cots_ref.at[2 * origin + 1 - x, rest_rows[part]]
             remote(block, block, q_send.at[part, origin], q_recv.at[part, origin], ctx_id(twin)).wait_recv()
     to_twin_first().wait_send()
     for origin in range(4):
-        for part in range(2):
+        for part in range(PARTS):
             to_twin_rest(origin, part).wait_send()
         for side in (1, -1):
 
             @pl.when(goes(side) & (origin <= z if side > 0 else origin >= z))
             def _():
-                for part in range(2):
+                for part in range(PARTS):
                     along(origin, side, part).wait_send()
                 along_first(origin, side).wait_send()
 
@@ -418,7 +419,8 @@
             pltpu.VMEM((2, rows, length), f32),
             pltpu.VMEM((rows, length), f32),
             dma((8,)), dma((8,)), dma((8,)), dma((8,)), dma((4,)), dma((2,)), dma((2,)), dma((1,)), dma((1,)),
-            dma((5,)), dma((2, 4)), dma((4,)), dma((2, 4)), dma((2, 2, 4)), dma((2, 4)), dma((1,)), dma((2, 4)),
+            dma((5,)), dma((PARTS, 4)), dma((4,)), dma((PARTS, 4)), dma((2, PARTS, 4)), dma((2, 4)), dma((1,)),
+            dma((PARTS, 4)),
             dma((8,)), dma((8,)), dma((8,)), dma((8,)), dma((3,)), dma((3,)),
         ],
         compiler_params=pltpu.CompilerParams(

time: 154 us -> 158 us (1.026)
  Pallas kernels: 124 us -> 127 us
    pallas_call x1, Pallas kernels: 124 us -> 127 us  [move_all(): pl.pallas_call(functools.partial(move_kernel, CUT), out_shape=(jax.ShapeD...]
where the time goes in v5:
time: 158 us
  Pallas kernels  127 us (80%)
  matrix products  19.1 us (12%)
  other arithmetic  7.68 us (5%)
  local copies, waits for them, and re-layouts  1.85 us (1%)
    pallas_call x1, Pallas kernels, move_all(): pl.pallas_call(functools.partial(move_kernel, CUT), out_shape=(jax.ShapeD...  127 us
    dot_general x1, matrix products, local(): jnp.dot(gated_rows, cotangent_all, preferred_element_type=jnp.float32)  10.6 us
    dot_general x1, matrix products, local(): jnp.einsum('gcs,gts->gct', mixed, kernel, precision=HIGH)  3.22 us

profile of v5, /device:TPU:24, one launch (start us, length us, event | category | flops | bytes accessed | tf_op | source)
XLA Modules:
  0.0 157.6 jit_solution(4607734868543836526)
XLA Ops:
  0.6 0.0 copy-start
  0.7 1.4 fusion.39
  2.8 0.7 convert_reduce_fusion
  3.5 0.6 slice.15
  4.1 0.7 convert_reduce_fusion.1
  4.8 0.7 compare_and_fusion
  5.6 0.7 neg.5
  6.2 0.1 exponential_select_fusion
  6.4 0.1 broadcast_in_dim.34.ahead_ref
  6.5 0.1 broadcast_in_dim.36.behind_ref
  6.6 1.4 fusion.14
  8.1 0.2 fusion.5
  8.3 0.3 convert_multiply_fusion.1
  8.6 3.2 %fusion.8 = f32[2,512,512]{2,1,0:T(8,128)} fusion(f32[2,512,512]{2,1,0:T(8,128)S(1)} %bitcast.15, f32[2,128,128]{1,2,0:T(8,128)S(1)} %slice.22, f32[2,256,128]{1,2,0:T(8,128)S(1)} %slice.21, f32[2,384,128]{1,2,0:T(8,128)S(1)} %slice.20, f32[2,512,128]{1,2,0:T(8,128)S(1)} %fusion.14, pred[512,512]{0,1:T(8,128)(4,1)S(1)} %fusion.5), kind=kOutput, calls=%fused_computation.21 | convolution fusion | flops 1617952768 | bytes 5767168 | tf_op jit(solution)/shard_map/gcs,gts->gct/dot_general | solution.py:500
  11.8 0.7 compare_convert_fusion
  12.5 1.0 fusion.18.part_ref
  13.6 0.1 exponential_multiply_fusion
  13.7 127.4 %move_all.1 = (bf16[8,512,1024]{2,1,0:T(8,128)(2,1)}, bf16[512,4096]{1,0:T(8,128)(2,1)}, bf16[8,128,512]{2,1,0:T(8,128)(2,1)}, bf16[128,4096]{1,0:T(8,128)(2,1)}...) custom-call(bf16[512,1024]{1,0:T(8,128)(2,1)} %cot_near.1, ...), custom_call_target="tpu_custom_call" | custom-call | bytes 300000000 | tf_op jit(solution)/shard_map/move_all/pallas_call | solution.py:397
  141.1 10.6 %convolution_multiply_fusion = f32[512,1024]{1,0:T(8,128)} fusion(bf16[512,4096]{1,0:T(8,128)(2,1)} %get-tuple-element.12, bf16[4096,1024]{1,0:T(8,128)(2,1)} %bitcast.19), kind=kOutput, calls=%fused_computation.17 | convolution fusion | flops 4295491584 | bytes 14680064 | tf_op jit(solution)/shard_map/dot_general | solution.py:523
  151.7 0.0 copy-done.4
  151.7 1.9 %fusion.6 = f32[2,512,512]{2,1,0:T(8,128)S(1)} fusion(f32[2,512,512]{2,1,0:T(8,128)S(1)} %bitcast.20, f32[2,128,128]{1,2,0:T(8,128)S(1)} %slice.22, f32[2,256,128]{1,2,0:T(8,128)S(1)} %slice.21, f32[2,384,128]{1,2,0:T(8,128)S(1)} %slice.20, f32[2,512,128]{1,2,0:T(8,128)S(1)} %fusion.14, pred[512,512]{0,1:T(8,128)(4,1)S(1)} %fusion.5), kind=kOutput, calls=%fused_computation.20 | convolution fusion | flops 1617952768 | bytes 5767168 | tf_op jit(solution)/shard_map/gct,gts->gcs/dot_general | solution.py:516
  153.6 1.0 convolution_add_fusion
  154.7 1.9 %fusion = (bf16[1024,512]{1,0:T(8,128)(2,1)}, bf16[1024,512]{1,0:T(8,128)(2,1)}) fusion(bf16[1024,512]{1,0:T(8,128)(2,1)S(1)} %copy-done.1, f32[2,512,512]{2,1,0:T(8,128)S(1)} %convolution_add_fusion, bf16[1024,512]{1,0:T(8,128)(2,1)S(1)} %copy-done), kind=kLoop, calls=%fused_computation.7 | loop fusion | flops 3145728 | bytes 6291456 | tf_op jit(solution)/shard_map/convert_element_type | solution.py:520
  156.6 1.0 copy.19
  (20 shorter events, 0.1 us)
Async XLA Ops:
  0.6 7.7 %copy-start = (bf16[1024,512]{1,0:T(8,128)(2,1)S(1)}, bf16[1024,512]{1,0:T(8,128)(2,1)}, u32[]{:S(2)}) copy-start(bf16[1024,512]{1,0:T(8,128)(2,1)} %param.10) | copy-start | bytes 3145732
  0.6 7.7 %copy-start.1 = (bf16[1024,512]{1,0:T(8,128)(2,1)S(1)}, bf16[1024,512]{1,0:T(8,128)(2,1)}, u32[]{:S(2)}) copy-start(bf16[1024,512]{1,0:T(8,128)(2,1)} %param.9) | copy-start | bytes 3145732
  11.8 1.7 %copy-start.3 = (f32[2,16]{1,0:T(2,128)S(1)}, f32[2,16]{1,0:T(2,128)}, u32[]{:S(2)}) copy-start(f32[2,16]{1,0:T(2,128)} %param.12) | copy-start | bytes 388
  141.1 10.6 %copy-start.4 = (f32[1024,512]{1,0:T(8,128)S(1)}, f32[1024,512]{1,0:T(8,128)}, u32[]{:S(2)}) copy-start(f32[1024,512]{1,0:T(8,128)} %get-tuple-element.10) | copy-start | bytes 6291460
  154.7 1.9 %copy-start.2 = (bf16[1024,512]{1,0:T(8,128)(2,1)S(1)}, bf16[1024,512]{1,0:T(8,128)(2,1)}, u32[]{:S(2)}) copy-start(bf16[1024,512]{1,0:T(8,128)(2,1)} %get-tuple-element.30) | copy-start | bytes 3145732
